TPU v7x, 128 devices: a whole 4x4x4 slice. The times are simulated.
128 devices in a mesh: chan: 16 (over z, y_lo, core), filt: 8 (over x, y_hi).
Axes of the slice: x: 4, y: 4 (y_hi: 2, y_lo: 2; y = y_hi * 2 + y_lo), z: 4, core: 2. Of those that a mesh axis runs over, the one named last changes fastest.
Arguments:
- inputs: bfloat16 [2048, 16, 1024], P('chan', 'filt'), may hold values from -6 to 6
- conv_kernel: bfloat16 [27, 2048, 128], P(None, 'chan'), may hold values from -0.109375 to 0.109375
- proj_weight: bfloat16 [2048, 2048], P('filt', 'chan'), may hold values from -0.1875 to 0.1875
- out_grad: bfloat16 [2048, 16, 1024], P('chan', 'filt'), may hold values from -6 to 6
Outputs:
- projected: bfloat16 [2048, 16, 1024], P('chan', 'filt')
- input_grad: bfloat16 [2048, 16, 1024], P('chan', 'filt')
- kernel_grad: float32 [27, 2048, 128], P(None, 'chan')
- weight_grad: float32 [2048, 2048], P('filt', 'chan')
All inputs are finite; a program needn't handle non-finite values.
Results may differ from a plain program's by a relative error of at most 0.018.
Values may be sent and summed in bfloat16 or wider, within the bound.
A program may use at most 128 MiB of HBM per device.

v0:
```python
import jax
import jax.numpy as jnp
from jax import lax
from jax.sharding import PartitionSpec as P

NY = 32
NZ = 32


def with_halo(array, sides, width):
    for axis, dim in sides:
        size, length = (lax.axis_size(axis), array.shape[dim])
        up = [(i, (i + 1) % size) for i in range(size - 1)]
        down = [(j, i) for i, j in up]
        last = lax.slice_in_dim(array, length - width, length, axis=dim)
        leading = lax.slice_in_dim(array, 0, width, axis=dim)
        before = lax.ppermute(last, axis, up)
        after = lax.ppermute(leading, axis, down)
        array = jnp.concatenate([before, array, after], axis=dim)
    return array


def activation(values):
    return jax.nn.gelu(values, approximate=True)


def tap_list():
    result = []
    for shift_a in (-1, 0, 1):
        for shift_b in (-1, 0, 1):
            for shift_c in (-1, 0, 1):
                result.append((shift_a, shift_b, shift_c))
    return result


def to_volume(block, width_in, planes):
    shaped = block.reshape(width_in, planes + 2, NY, NZ)
    return jnp.pad(shaped, ((0, 0), (0, 0), (1, 1), (1, 1)))


def body(inputs, conv_kernel, proj_weight, out_grad):
    width_in, planes, columns = inputs.shape
    cell_count = planes * columns
    padded_in = with_halo(inputs, (("filt", 1),), 1)
    volume_in = to_volume(padded_in, width_in, planes)
    windows = []
    pre = jnp.zeros((width_in, cell_count), jnp.float32)
    for tap, (shift_a, shift_b, shift_c) in enumerate(tap_list()):
        window = volume_in[
            :,
            1 + shift_a : 1 + shift_a + planes,
            1 + shift_b : 1 + shift_b + NY,
            1 + shift_c : 1 + shift_c + NZ,
        ].reshape(width_in, cell_count)
        windows.append(window)
        pre = pre + jnp.dot(conv_kernel[tap], window, preferred_element_type=jnp.float32)
    hidden = activation(pre).astype(jnp.bfloat16)
    w_cols = lax.all_gather(proj_weight, "filt", axis=0, tiled=True)
    filters = w_cols.shape[0]
    portion = w_cols
    projected = lax.psum_scatter(
        jnp.dot(portion, hidden, preferred_element_type=jnp.float32)
        .reshape(filters // lax.axis_size("chan") * lax.axis_size("chan"), planes, columns)
        .astype(jnp.bfloat16),
        "chan",
        scatter_dimension=0,
        tiled=True,
    )
    portion = lax.all_gather(out_grad, "chan", axis=0, tiled=True)
    row_count = portion.shape[0]
    grad_rows = portion.reshape(row_count, cell_count)
    hidden_grad = lax.dot_general(
        w_cols, grad_rows, (((0,), (0,)), ((), ())), preferred_element_type=jnp.float32
    )
    partial_value = lax.dot_general(
        grad_rows, hidden, (((1,), (1,)), ((), ())), preferred_element_type=jnp.float32
    )
    weight_part = partial_value
    hidden_grad, weight_part = (hidden_grad, weight_part)
    weight_grad = lax.psum_scatter(
        weight_part.astype(jnp.bfloat16), "filt", scatter_dimension=0, tiled=True
    ).astype(jnp.float32)
    derivative = jax.jvp(activation, (pre,), (jnp.ones_like(pre),))[1]
    conv_grad = (hidden_grad * derivative).astype(jnp.bfloat16)
    padded_grad = with_halo(conv_grad.reshape(width_in, planes, columns), (("filt", 1),), 1)
    volume_grad = to_volume(padded_grad, width_in, planes)
    input_grad = jnp.zeros((width_in, cell_count), jnp.float32)
    kernel_parts = []
    for tap, (shift_a, shift_b, shift_c) in enumerate(tap_list()):
        moved = volume_grad[
            :,
            1 - shift_a : 1 - shift_a + planes,
            1 - shift_b : 1 - shift_b + NY,
            1 - shift_c : 1 - shift_c + NZ,
        ].reshape(width_in, cell_count)
        input_grad = input_grad + lax.dot_general(
            conv_kernel[tap], moved, (((0,), (0,)), ((), ())), preferred_element_type=jnp.float32
        )
        kernel_parts.append(
            lax.dot_general(
                conv_grad,
                windows[tap],
                (((1,), (1,)), ((), ())),
                preferred_element_type=jnp.float32,
            )
        )
    kernel_grad = lax.psum(jnp.stack(kernel_parts, axis=0).astype(jnp.bfloat16), "filt").astype(
        jnp.float32
    )
    input_grad = input_grad.reshape(width_in, planes, columns).astype(jnp.bfloat16)
    return (projected, input_grad, kernel_grad, weight_grad)


def solution(mesh):
    in_specs = (
        P("chan", "filt", None),
        P(None, "chan", None),
        P("filt", "chan"),
        P("chan", "filt", None),
    )
    out_specs = (
        P("chan", "filt", None),
        P("chan", "filt", None),
        P(None, "chan", None),
        P("filt", "chan"),
    )
    return jax.shard_map(body, mesh=mesh, in_specs=in_specs, out_specs=out_specs, check_vma=False)
```

profile of v0, /device:TPU:0, one launch (start us, length us, event | category | flops | bytes accessed | tf_op | source)
XLA Modules:
  0.0 471.5 jit_solution(6132504420923754638)
XLA Ops:
  8.0 1.4 copy.19
  9.4 5.2 %collective-permute-start = (bf16[128,1,1024]{0,2,1:T(8,128)(2,1)S(1)}, bf16[128,1,1024]{0,2,1:T(8,128)(2,1)S(1)}, u32[]{:S(2)}, u32[]{:S(2)}) collective-permute-start(bf16[128,1,1024]{0,2,1:T(8,128)(2,1)S(1)} %get-tuple-element.71), channel_id=1, source_target_pairs={{0,1},{1,2},{2,3},{3,4},{4,5},{5,6},{6,7},{8,9},{9,10},{10,11},{11... | collective-permute-start | bytes 786440 | tf_op jit(solution)/shard_map/ppermute | solution.py:17
  14.6 1.3 collective-permute-start.1
  15.9 44.4 %all_gather.6 = bf16[2048,128]{1,0:T(8,128)(2,1)S(1)} all-gather(bf16[256,128]{1,0:T(8,128)(2,1)S(1)} %copy-done.52), channel_id=1, replica_groups=mesh['chan'=16,'filt'=8] {'filt'}, dimensions={0}, use_global_device_ids=true | all-gather | bytes 589824 | tf_op jit(solution)/shard_map/all_gather | solution.py:58
  60.4 1.0 pad_slice_fusion.1
  61.9 3.2 pad_slice_fusion
  73.4 5.7 %convolution_convert_fusion = bf16[2048,2048]{1,0:T(8,128)(2,1)} fusion(bf16[2048,128]{1,0:T(8,128)(2,1)S(1)} %all_gather.6, f32[128,2048]{0,1:T(8,128)S(1)} %fusion.14), kind=kOutput, calls=%fused_computation | convolution fusion | flops 1080295424 | bytes 9961472 | tf_op jit(solution)/shard_map/dot_general | solution.py:62
  79.1 21.5 %copy.22 = bf16[2048,2,1024]{2,1,0:T(2,128)(2,1)} copy(bf16[2048,2,1024]{0,2,1:T(8,128)(2,1)} %bitcast.511) | data formatting | bytes 16777216 | tf_op jit(solution)/shard_map/convert_element_type | solution.py:64
  102.5 10.3 %copy.27 = bf16[256,8,2,1024]{3,1,2,0:T(8,128)(2,1)} copy(bf16[256,8,2,1024]{3,2,1,0:T(2,128)(2,1)} %bitcast.514) | data formatting | bytes 16777216
  112.8 7.0 %fusion.25 = bf16[128,2048]{0,1:T(8,128)(2,1)S(1)} fusion(bf16[2048,128]{1,0:T(8,128)(2,1)S(1)} %copy-done.51, bf16[2048,2048]{1,0:T(8,128)(2,1)} %bitcast.515, f32[128,2048]{0,1:T(8,128)S(1)} %fusion.14), kind=kOutput, calls=%fused_computation.84 | convolution fusion | flops 1078460416 | bytes 10485760 | tf_op jit(solution)/shard_map/dot_general | solution.py:72
  120.7 1.0 fusion.34
  121.7 1.0 fusion.36
  126.5 1.0 fusion.46
  130.4 1.0 fusion.54
  133.3 11.4 %fusion.60 = bf16[27,128,128]{2,1,0:T(8,128)(2,1)} fusion(bf16[27,128,128]{2,1,0:T(8,128)(2,1)} %fusion.58, bf16[128,2048]{0,1:T(8,128)(2,1)S(1)} %fusion.25, bf16[128,2048]{0,1:T(8,128)(2,1)S(1)} %bitcast.548), kind=kOutput, calls=%fused_computation.174 | convolution fusion | flops 67125248 | bytes 1081344 | tf_op jit(solution)/shard_map/dot_general | solution.py:100
  144.7 1.0 fusion.62
  146.7 1.0 fusion.66
  147.7 1.0 fusion.68
  149.6 1.0 fusion.72
  150.6 1.0 fusion.74
  156.4 139.6 %all-reduce.8.cloned.1.call-done = bf16[2048,2,1024]{2,1,0:T(2,128)(2,1)} async-done(((bf16[2048,2,1024]{2,1,0:T(2,128)(2,1)}), bf16[2048,2,1024]{2,1,0:T(2,128)(2,1)}) %all-reduce.8.cloned.1.call-update) | async-done | bytes 8388624
  296.0 2.2 constant_dynamic-slice_fusion
  298.3 4.6 collective-permute-start.2
  302.9 1.3 collective-permute-start.3
  304.2 7.2 %fusion.27 = bf16[2048,128]{0,1:T(8,128)(2,1)} fusion(bf16[2048,2048]{1,0:T(8,128)(2,1)} %bitcast.516, f32[128,2048]{0,1:T(8,128)S(1)} %fusion.14), kind=kOutput, calls=%fused_computation.86 | convolution fusion | flops 1076363264 | bytes 9961472 | tf_op jit(solution)/shard_map/dot_general | solution.py:75
  311.4 5.5 %collective-permute-done.2 = bf16[128,1,1024]{0,2,1:T(8,128)(2,1)S(1)} collective-permute-done((bf16[128,1,1024]{0,2,1:T(8,128)(2,1)S(1)}, bf16[128,1,1024]{0,2,1:T(8,128)(2,1)S(1)}, u32[]{:S(2)}, u32[]{:S(2)}) %collective-permute-start.2) | collective-permute-done | bytes 262176 | tf_op jit(solution)/shard_map/ppermute | solution.py:17
  318.1 2.7 fusion.205
  328.5 1.1 copy.24
  329.6 61.0 %all-reduce.6.cloned.1.call-done = bf16[27,128,128]{2,1,0:T(8,128)(2,1)} async-done(((bf16[27,128,128]{2,1,0:T(8,128)(2,1)}), bf16[27,128,128]{2,1,0:T(8,128)(2,1)}) %all-reduce.6.cloned.1.call-update) | async-done | bytes 884752 | tf_op jit(solution)/shard_map/psum | solution.py:107
  390.6 2.6 convert_element_type.44
  393.2 69.9 %reduce-scatter.2.cloned.1.call-done = bf16[256,128]{0,1:T(8,128)(2,1)} async-done(((bf16[2048,128]{0,1:T(8,128)(2,1)}), bf16[256,128]{0,1:T(8,128)(2,1)}) %reduce-scatter.2.cloned.1.call-update) | async-done | bytes 65552 | tf_op jit(solution)/shard_map/reduce_scatter | solution.py:80
  463.2 1.6 copy.25
  (198 shorter events, 35.6 us)
Async XLA Ops:
  7.2 8.7 %copy-start.52 = (bf16[256,128]{1,0:T(8,128)(2,1)S(1)}, bf16[256,128]{1,0:T(8,128)(2,1)}, u32[]{:S(2)}) copy-start(bf16[256,128]{1,0:T(8,128)(2,1)} %param.6) | copy-start | bytes 196612
  7.2 95.3 %all-gather.2.cloned.1.call-start = ((), (), s32[]{:S(2)}) async-start(), calls=%async_computation.1 | async-start | bytes 8912896 | tf_op jit(solution)/shard_map/all_gather | solution.py:69
  7.9 288.1 %all-reduce.8.cloned.1.call-start = ((), (), s32[]{:S(2)}) async-start(), calls=%async_computation.4 | async-start | bytes 16777216
  9.4 50.9 %collective-permute-start = (bf16[128,1,1024]{0,2,1:T(8,128)(2,1)S(1)}, bf16[128,1,1024]{0,2,1:T(8,128)(2,1)S(1)}, u32[]{:S(2)}, u32[]{:S(2)}) collective-permute-start(bf16[128,1,1024]{0,2,1:T(8,128)(2,1)S(1)} %get-tuple-element.71), channel_id=1, source_target_pairs={{0,1},{1,2},{2,3},{3,4},{4,5},{5,6},{6,7},{8,9},{9,10},{10,11},{11... | collective-permute-start | bytes 786440 | tf_op jit(solution)/shard_map/ppermute | solution.py:17
  14.6 45.7 %collective-permute-start.1 = (bf16[128,1,1024]{0,2,1:T(8,128)(2,1)S(1)}, bf16[128,1,1024]{0,2,1:T(8,128)(2,1)S(1)}, u32[]{:S(2)}, u32[]{:S(2)}) collective-permute-start(bf16[128,1,1024]{0,2,1:T(8,128)(2,1)S(1)} %get-tuple-element.72), channel_id=1, source_target_pairs={{1,0},{2,1},{3,2},{4,3},{5,4},{6,5},{7,6},{9,8},{10,9},{11,10},{12... | collective-permute-start | bytes 786440 | tf_op jit(solution)/shard_map/ppermute | solution.py:18
  60.3 13.1 %copy-start.50 = (bf16[2048,128]{1,0:T(8,128)(2,1)}, bf16[2048,128]{1,0:T(8,128)(2,1)S(1)}, u32[]{:S(2)}) copy-start(bf16[2048,128]{1,0:T(8,128)(2,1)S(1)} %all_gather.6) | copy-start | bytes 1572868
  61.4 4.8 %copy-start.8 = (bf16[128,2,32,32]{0,3,2,1:T(8,128)(2,1)}, bf16[128,2,32,32]{0,3,2,1:T(8,128)(2,1)S(1)}, u32[]{:S(2)}) copy-start(bf16[128,2,32,32]{0,3,2,1:T(8,128)(2,1)S(1)} %get-tuple-element.65) | copy-start | bytes 1572868
  61.4 7.6 %copy-start.6 = (bf16[128,2,32,32]{0,3,2,1:T(8,128)(2,1)}, bf16[128,2,32,32]{0,3,2,1:T(8,128)(2,1)S(1)}, u32[]{:S(2)}) copy-start(bf16[128,2,32,32]{0,3,2,1:T(8,128)(2,1)S(1)} %get-tuple-element.64) | copy-start | bytes 1572868
  61.5 10.1 %copy-start.4 = (bf16[128,2,32,32]{0,3,2,1:T(8,128)(2,1)}, bf16[128,2,32,32]{0,3,2,1:T(8,128)(2,1)S(1)}, u32[]{:S(2)}) copy-start(bf16[128,2,32,32]{0,3,2,1:T(8,128)(2,1)S(1)} %get-tuple-element.60) | copy-start | bytes 1572868
  61.5 10.4 %copy-start.2 = (bf16[128,2,32,32]{0,3,2,1:T(8,128)(2,1)}, bf16[128,2,32,32]{0,3,2,1:T(8,128)(2,1)S(1)}, u32[]{:S(2)}) copy-start(bf16[128,2,32,32]{0,3,2,1:T(8,128)(2,1)S(1)} %get-tuple-element.63) | copy-start | bytes 1572868
  61.5 10.7 %copy-start = (bf16[128,2,32,32]{0,3,2,1:T(8,128)(2,1)}, bf16[128,2,32,32]{0,3,2,1:T(8,128)(2,1)S(1)}, u32[]{:S(2)}) copy-start(bf16[128,2,32,32]{0,3,2,1:T(8,128)(2,1)S(1)} %get-tuple-element.61) | copy-start | bytes 1572868
  65.2 2.9 copy-start.30
  65.2 3.2 copy-start.28
  65.2 3.5 copy-start.26
  65.2 4.2 copy-start.24
  65.2 4.5 copy-start.22
  65.2 4.8 %copy-start.20 = (bf16[128,2,32,32]{0,3,2,1:T(8,128)(2,1)}, bf16[128,2,32,32]{0,3,2,1:T(8,128)(2,1)S(1)}, u32[]{:S(2)}) copy-start(bf16[128,2,32,32]{0,3,2,1:T(8,128)(2,1)S(1)} %get-tuple-element.54) | copy-start | bytes 1572868
  65.2 5.1 %copy-start.18 = (bf16[128,2,32,32]{0,3,2,1:T(8,128)(2,1)}, bf16[128,2,32,32]{0,3,2,1:T(8,128)(2,1)S(1)}, u32[]{:S(2)}) copy-start(bf16[128,2,32,32]{0,3,2,1:T(8,128)(2,1)S(1)} %get-tuple-element.55) | copy-start | bytes 1572868
  65.3 5.4 %copy-start.16 = (bf16[128,2,32,32]{0,3,2,1:T(8,128)(2,1)}, bf16[128,2,32,32]{0,3,2,1:T(8,128)(2,1)S(1)}, u32[]{:S(2)}) copy-start(bf16[128,2,32,32]{0,3,2,1:T(8,128)(2,1)S(1)} %get-tuple-element.56) | copy-start | bytes 1572868
  65.3 5.7 %copy-start.14 = (bf16[128,2,32,32]{0,3,2,1:T(8,128)(2,1)}, bf16[128,2,32,32]{0,3,2,1:T(8,128)(2,1)S(1)}, u32[]{:S(2)}) copy-start(bf16[128,2,32,32]{0,3,2,1:T(8,128)(2,1)S(1)} %get-tuple-element.57) | copy-start | bytes 1572868
  65.3 6.0 %copy-start.12 = (bf16[128,2,32,32]{0,3,2,1:T(8,128)(2,1)}, bf16[128,2,32,32]{0,3,2,1:T(8,128)(2,1)S(1)}, u32[]{:S(2)}) copy-start(bf16[128,2,32,32]{0,3,2,1:T(8,128)(2,1)S(1)} %get-tuple-element.58) | copy-start | bytes 1572868
  65.3 7.8 %copy-start.10 = (bf16[128,2,32,32]{0,3,2,1:T(8,128)(2,1)}, bf16[128,2,32,32]{0,3,2,1:T(8,128)(2,1)S(1)}, u32[]{:S(2)}) copy-start(bf16[128,2,32,32]{0,3,2,1:T(8,128)(2,1)S(1)} %get-tuple-element.40) | copy-start | bytes 1572868
  100.6 290.1 %all-reduce.6.cloned.1.call-start = ((), (), s32[]{:S(2)}) async-start(), calls=%async_computation.2 | async-start | bytes 1769472 | tf_op jit(solution)/shard_map/psum | solution.py:107
  102.5 10.3 %copy-start.51 = (bf16[2048,128]{1,0:T(8,128)(2,1)S(1)}, bf16[2048,128]{1,0:T(8,128)(2,1)}, u32[]{:S(2)}) copy-start(bf16[2048,128]{1,0:T(8,128)(2,1)} %copy-done.50) | copy-start | bytes 1572868
  112.8 7.9 %copy-start.47 = (bf16[128,2,32,32]{0,3,2,1:T(8,128)(2,1)S(1)}, bf16[128,2,32,32]{0,3,2,1:T(8,128)(2,1)}, u32[]{:S(2)}) copy-start(bf16[128,2,32,32]{0,3,2,1:T(8,128)(2,1)} %copy-done.46) | copy-start | bytes 1572868
  131.4 13.3 %copy-start.23 = (bf16[128,2,32,32]{0,3,2,1:T(8,128)(2,1)S(1)}, bf16[128,2,32,32]{0,3,2,1:T(8,128)(2,1)}, u32[]{:S(2)}) copy-start(bf16[128,2,32,32]{0,3,2,1:T(8,128)(2,1)} %copy-done.22) | copy-start | bytes 1572868
  132.4 13.3 %copy-start.21 = (bf16[128,2,32,32]{0,3,2,1:T(8,128)(2,1)S(1)}, bf16[128,2,32,32]{0,3,2,1:T(8,128)(2,1)}, u32[]{:S(2)}) copy-start(bf16[128,2,32,32]{0,3,2,1:T(8,128)(2,1)} %copy-done.20) | copy-start | bytes 1572868
  133.3 13.3 %copy-start.19 = (bf16[128,2,32,32]{0,3,2,1:T(8,128)(2,1)S(1)}, bf16[128,2,32,32]{0,3,2,1:T(8,128)(2,1)}, u32[]{:S(2)}) copy-start(bf16[128,2,32,32]{0,3,2,1:T(8,128)(2,1)} %copy-done.18) | copy-start | bytes 1572868
  145.7 2.9 copy-start.15
  156.4 306.8 %reduce-scatter.2.cloned.1.call-start = ((), (), s32[]{:S(2)}) async-start(), calls=%async_computation.3 | async-start | bytes 589824 | tf_op jit(solution)/shard_map/reduce_scatter | solution.py:80
  298.3 18.7 %collective-permute-start.2 = (bf16[128,1,1024]{0,2,1:T(8,128)(2,1)S(1)}, bf16[128,1,1024]{0,2,1:T(8,128)(2,1)S(1)}, u32[]{:S(2)}, u32[]{:S(2)}) collective-permute-start(bf16[128,1,1024]{0,2,1:T(8,128)(2,1)S(1)} %get-tuple-element.69), channel_id=1, source_target_pairs={{0,1},{1,2},{2,3},{3,4},{4,5},{5,6},{6,7},{8,9},{9,10},{10,11},{11... | collective-permute-start | bytes 786440 | tf_op jit(solution)/shard_map/ppermute | solution.py:17
  302.9 14.1 %collective-permute-start.3 = (bf16[128,1,1024]{0,2,1:T(8,128)(2,1)S(1)}, bf16[128,1,1024]{0,2,1:T(8,128)(2,1)S(1)}, u32[]{:S(2)}, u32[]{:S(2)}) collective-permute-start(bf16[128,1,1024]{0,2,1:T(8,128)(2,1)S(1)} %get-tuple-element.70), channel_id=1, source_target_pairs={{1,0},{2,1},{3,2},{4,3},{5,4},{6,5},{7,6},{9,8},{10,9},{11,10},{12... | collective-permute-start | bytes 786440 | tf_op jit(solution)/shard_map/ppermute | solution.py:18
  (30 other events, 73.3 us)
Sparse Core Ops, SparseCore 0:
  9.7 67.8 all-gather.1
  100.7 195.2 all-reduce.7
  299.1 91.4 all-reduce.5
  394.5 68.6 reduce-scatter.1
where the time goes:
time: 481 us; the launch traced here: 471 us
  waiting for transfers between devices  277 us (58%)
  matrix products  71.8 us (15%)
  local copies, waits for them, and re-layouts  46.7 us (10%)
  blocking collectives  44.4 us (9%)
  between operations  15.6 us (3%)
  starting transfers between devices  12.8 us (3%)
    unnamed x5, waiting for transfers between devices  140 us
    reduce_scatter x1, waiting for transfers between devices, body(): lax.psum_scatter(weight_part.astype(jnp.bfloat16), 'filt', scatter_dimens...  69.9 us
    psum x1, waiting for transfers between devices, body(): lax.psum(jnp.stack(kernel_parts, axis=0).astype(jnp.bfloat16), 'filt')  61 us
    all_gather x1, blocking collectives, body(): w_cols = lax.all_gather(proj_weight, 'filt', axis=0, tiled=True)  44.4 us
    dot_general x27, matrix products, body(): lax.dot_general(conv_grad, windows[tap], (((1,), (1,)), ((), ())), prefer...  36.5 us
    convert_element_type x1, local copies, waits for them, and re-layouts, body(): projected = lax.psum_scatter(jnp.dot(portion, hidden, preferred_element_t...  21.5 us
    unnamed x114, local copies, waits for them, and re-layouts  17.9 us
    ppermute x2, starting transfers between devices, with_halo(): before = lax.ppermute(last, axis, up)  9.84 us
  transfers between devices with their start and end apart: 8, of which 4 were waited for; matrix products, arithmetic and copies ran while one was open for 25% of the time, Pallas kernels for 0%

commit v1 on v0

v1 whole, which is shorter than its diff:
```python
import jax
import jax.numpy as jnp
from jax import lax
from jax.experimental import pallas as pl
from jax.experimental.pallas import tpu as pltpu
from jax.sharding import PartitionSpec as P

MESH = pl.DeviceIdType.MESH
F32 = jnp.float32
BF16 = jnp.bfloat16
NN = (((1,), (0,)), ((), ()))
NT = (((1,), (1,)), ((), ()))
N_SEMS = 128


def dot(a, b, dims):
    return lax.dot_general(a, b, dims, preferred_element_type=F32)


def kernel(
    x_ref, k_ref, w_ref, o_ref,
    p_out, ig_out, kg_out, wg_out,
    obuf, xhalo, x3t, k3, wbuf, wt, hown, hbuf, der,
    pbuf, r1, r2, r3, p4, r4,
    ghb, ghs, ghr, cg, cgt, chalo, c3t,
    wgf, wgs, wgr, wgp, wgq,
    kgb, kgr, kgs, kgall,
    ssem, rsem,
):
    ch = lax.axis_index("chan")
    fi = lax.axis_index("filt")
    co = ch % 2
    q = ch // 2
    yl = q % 2
    z = q // 2
    sib = ch + 1 - 2 * co
    zp = (ch + 4) % 16
    zm = (ch + 12) % 16
    yn = ch + 2 - 4 * yl
    own, oth = co, 1 - co
    flip = 1 - 2 * yl
    q_zp = ((z + 1) % 4) * 2 + yl
    q_zm = ((z + 3) % 4) * 2 + yl
    q_z2 = ((z + 2) % 4) * 2 + yl
    others = [(fi + d) % 8 for d in range(1, 8)]
    sent = []

    def send(src, dst, chan_id, filt_id=None):
        i = len(sent)
        copy = pltpu.make_async_remote_copy(
            src_ref=src, dst_ref=dst, send_sem=ssem.at[i], recv_sem=rsem.at[i],
            device_id=(chan_id, fi if filt_id is None else filt_id), device_id_type=MESH,
        )
        copy.start()
        sent.append(copy)
        return copy

    barrier = pltpu.get_barrier_semaphore()
    for c in (sib, zp, zm, yn):
        pl.semaphore_signal(barrier, inc=1, device_id=(c, fi), device_id_type=MESH)
    for f in others:
        pl.semaphore_signal(barrier, inc=1, device_id=(ch, f), device_id_type=MESH)
    pl.semaphore_wait(barrier, 11)

    c1 = send(o_ref.at[oth], obuf.at[q, own], sib)
    a_p = send(o_ref.at[own], obuf.at[q, own], zp)
    a_m = send(o_ref.at[own], obuf.at[q, own], zm)
    a_y = send(o_ref.at[own], obuf.at[q, own], yn)
    x_up = send(x_ref.at[1], xhalo.at[0], ch, (fi + 1) % 8)
    x_dn = send(x_ref.at[0], xhalo.at[1], ch, (fi + 7) % 8)
    w_own = pl.ds(pl.multiple_of(fi * 256, 256), 256)
    w_out = [send(w_ref, wbuf.at[own, w_own], ch, f) for f in others]
    w_sib = [send(w_ref, wbuf.at[own, w_own], sib)]

    wbuf[own, w_own] = w_ref[...]
    obuf[q, own] = o_ref[own]
    for t in range(27):
        k3[:, t * 128 : (t + 1) * 128] = k_ref[t]

    def spread(dst, at, src, low, keep):
        edge = jnp.zeros((32, 384), BF16)
        dst[at, 0:32] = edge
        dst[at, 1056:1088] = edge

        @pl.loop(0, 4)
        def _(i):
            rows = pl.ds(pl.multiple_of(i * 256, 256), 256)
            v = src[rows].astype(F32) * keep
            r = lax.broadcasted_iota(jnp.int32, (256, 128), 0) % 32
            prev = jnp.where(r == 0, 0.0, pltpu.roll(v, 1, 0))
            after = jnp.where(r == 31, 0.0, pltpu.roll(v, 255, 0))
            left, right = (prev, after) if low else (after, prev)
            to = pl.ds(pl.multiple_of(i * 256 + 32, 32), 256)
            dst[at, to, 0:128] = left.astype(BF16)
            dst[at, to, 128:256] = v.astype(BF16)
            dst[at, to, 256:384] = right.astype(BF16)

    one = jnp.float32(1.0)
    first = jnp.where(fi == 0, 0.0, 1.0).astype(F32)
    last = jnp.where(fi == 7, 0.0, 1.0).astype(F32)
    spread(x3t, 1, x_ref.at[0], True, one)
    spread(x3t, 2, x_ref.at[1], True, one)

    c1.wait_recv()
    b_y = send(obuf.at[q, oth], obuf.at[q, oth], yn)
    b_p = send(obuf.at[q, oth], obuf.at[q, oth], zp)
    b_m = send(obuf.at[q, oth], obuf.at[q, oth], zm)

    for d, c in enumerate(w_out):
        c.wait_recv()
        src = (fi + 7 - d) % 8
        rows = pl.ds(pl.multiple_of(src * 256, 256), 256)
        w_sib.append(send(wbuf.at[own, rows], wbuf.at[own, rows], sib))

    x_up.wait_recv()
    x_dn.wait_recv()
    spread(x3t, 0, xhalo.at[0], True, first)
    spread(x3t, 3, xhalo.at[1], True, last)

    lower, upper = pl.ds(0, 64), pl.ds(64, 64)
    a_p.wait_recv()
    af_p = send(obuf.at[q_zm, own, lower], obuf.at[q_zm, own, lower], zp)
    ay_m = send(obuf.at[q_zm, own], obuf.at[q_zm, own], yn)
    a_m.wait_recv()
    af_m = send(obuf.at[q_zp, own, upper], obuf.at[q_zp, own, upper], zm)
    ay_p = send(obuf.at[q_zp, own], obuf.at[q_zp, own], yn)

    def convolve(plane, count, start):
        @pl.loop(start, start + count)
        def _(i):
            cols = pl.ds(pl.multiple_of(i * 256, 256), 256)
            wins = [
                x3t[plane + a, pl.ds(pl.multiple_of(i * 256 + 32 * b, 32), 256)]
                for a in range(3) for b in range(3)
            ]
            v = dot(k3[...], jnp.concatenate(wins, axis=1), NT)
            s = 0.7978845608028654
            sq = v * v
            t = jnp.tanh(s * (v + 0.044715 * sq * v))
            hown[plane, :, cols] = (0.5 * v * (1.0 + t)).astype(BF16)
            der[plane, :, cols] = 0.5 * (1.0 + t) + 0.5 * v * (1.0 - t * t) * (
                s * (1.0 + 3 * 0.044715 * sq)
            )

    convolve(oth, 2, 0)
    b_y.wait_recv()
    b2_p = send(obuf.at[q + flip, oth], obuf.at[q + flip, oth], zp)
    b2_m = send(obuf.at[q + flip, oth], obuf.at[q + flip, oth], zm)
    convolve(oth, 2, 2)
    h_x = send(hown.at[oth], hbuf.at[own], sib)
    b_p.wait_recv()
    bf_p = send(obuf.at[q_zm, oth, lower], obuf.at[q_zm, oth, lower], zp)
    b_m.wait_recv()
    bf_m = send(obuf.at[q_zp, oth, upper], obuf.at[q_zp, oth, upper], zm)
    convolve(own, 2, 0)
    af_p.wait_recv()
    af_m.wait_recv()
    ay_2 = send(obuf.at[q_z2, own], obuf.at[q_z2, own], yn)
    convolve(own, 2, 2)
    hbuf[own] = hown[own]
    b2_p.wait_recv()
    b2f_p = send(obuf.at[q_zm + flip, oth, lower], obuf.at[q_zm + flip, oth, lower], zp)
    b2_m.wait_recv()
    b2f_m = send(obuf.at[q_zp + flip, oth, upper], obuf.at[q_zp + flip, oth, upper], zm)

    for c in w_sib:
        c.wait_recv()

    @pl.loop(0, 8)
    def _(j):
        rows = pl.ds(pl.multiple_of(j * 256, 256), 256)
        for half in range(2):
            block = wbuf[half, rows].astype(F32)
            wt[half * 128 : (half + 1) * 128, rows] = block.T.astype(BF16)

    h_x.wait_recv()

    def project(at):
        rows = pl.ds(pl.multiple_of(at * 256, 256), 256)
        w = jnp.concatenate([wbuf[0, rows], wbuf[1, rows]], axis=1)

        @pl.loop(0, 4)
        def _(i):
            cols = pl.ds(pl.multiple_of(i * 256, 256), 256)
            h = jnp.concatenate([hbuf[0, :, cols], hbuf[1, :, cols]], axis=0)
            v = dot(w, h, NN).astype(BF16)
            pbuf[at, 0, :, cols] = v[:128]
            pbuf[at, 1, :, cols] = v[128:]

    far = (q_z2, q_z2 + flip)
    up = (q_zp, q_zp + flip)
    down = (q_zm, q_zm + flip)
    here = (q, q + flip)
    for at in far:
        project(at)
    s1 = []
    for i in range(2):
        s1.append((
            send(pbuf.at[far[i], 0], r1.at[0, i], zp),
            send(pbuf.at[far[i], 1], r1.at[1, i], zm),
        ))
    for at in up + down + here:
        project(at)

    for c in (a_y, ay_m, ay_p, ay_2, bf_p, bf_m, b2f_p, b2f_m):
        c.wait_recv()

    @pl.loop(0, 4)
    def _(i):
        cols = pl.ds(pl.multiple_of(i * 256, 256), 256)
        o = obuf[:, :, :, cols].reshape(2048, 256)
        v = dot(wt[...], o, NN)
        ghb[0, :, cols] = v[:128]
        ghb[1, :, cols] = v[128:]

    ghs[...] = ghb[oth].astype(BF16)
    g_x = send(ghs, ghr, sib)

    s2 = []
    for i in range(2):
        for side, blocks in ((0, up), (1, down)):
            s1[i][side].wait_recv()

            pbuf[blocks[i], side] = (
                pbuf[blocks[i], side].astype(F32) + r1[side, i].astype(F32)
            ).astype(BF16)
        s2.append((
            send(pbuf.at[up[i]], r2.at[0, i], zp),
            send(pbuf.at[down[i]], r2.at[1, i], zm),
        ))

    cg[own] = (ghb[own] * der[own]).astype(BF16)
    g_x.wait_recv()
    cg[oth] = (ghr[...].astype(F32) * der[oth]).astype(BF16)

    for plane in range(2):
        @pl.loop(0, 4)
        def _(i):
            cols = pl.ds(pl.multiple_of(i * 256, 256), 256)
            cgt[plane, cols] = cg[plane, :, cols].astype(F32).T.astype(BF16)

    g_up = send(cgt.at[1], chalo.at[0], ch, (fi + 1) % 8)
    g_dn = send(cgt.at[0], chalo.at[1], ch, (fi + 7) % 8)

    ks = []
    for a in range(3):
        @pl.loop(0, 3)
        def _(b):
            rows = pl.ds(pl.multiple_of(32 * b, 32), 1024)
            v = dot(cg[0], x3t[a, rows], NN) + dot(cg[1], x3t[a + 1, rows], NN)
            for c in range(3):
                to = pl.ds(pl.multiple_of((3 * b + c) * 128, 128), 128)
                kgb[a, to] = v[:, c * 128 : (c + 1) * 128].astype(BF16)

        ks.append([
            send(kgb.at[a, pl.ds(pl.multiple_of(f * 144, 16), 144)], kgr.at[a, fi], ch, f)
            for f in others
        ])

    @pl.loop(0, 8)
    def _(j):
        h = jnp.concatenate([hbuf[0], hbuf[1]], axis=0)
        v = dot(obuf[j].reshape(256, 1024), h, NT)
        lo, hi = v[:, :128], v[:, 128:]
        wgf[j] = jnp.where(co == 0, lo, hi)
        wgs[j] = jnp.where(co == 0, hi, lo).astype(BF16)

    wg_x = send(wgs, wgr, sib)

    spread(c3t, 1, cgt.at[0], False, one)
    spread(c3t, 2, cgt.at[1], False, one)

    for i in range(2):
        s2[i][0].wait_recv()
        s2[i][1].wait_recv()
    pbuf[here[1]] = (
        pbuf[here[1]].astype(F32) + r2[0, 1].astype(F32) + r2[1, 1].astype(F32)
    ).astype(BF16)
    s3 = send(pbuf.at[here[1]], r3, yn)

    wg_x.wait_recv()
    wgf[...] = wgf[...] + wgr[...].astype(F32)
    wgp[...] = wgf[...].astype(BF16)
    wq = [send(wgp.at[f], wgq.at[fi], ch, f) for f in others]

    g_up.wait_recv()
    g_dn.wait_recv()
    spread(c3t, 0, chalo.at[0], False, first)
    spread(c3t, 3, chalo.at[1], False, last)

    def back(plane):
        @pl.loop(0, 4)
        def _(i):
            wins = [
                c3t[plane + 2 - a, pl.ds(pl.multiple_of(i * 256 + 32 * (2 - b), 32), 256)]
                for a in range(3) for b in range(3)
            ]
            v = dot(jnp.concatenate(wins, axis=1), k_ref[...].reshape(3456, 128), NN)
            rows = pl.ds(pl.multiple_of(i * 256, 256), 256)
            ig_out[plane, rows] = v.astype(BF16)

    own_rows = pl.ds(pl.multiple_of(fi * 144, 16), 144)

    def reduce_kernel(a):
        total = kgb[a, own_rows].astype(F32)
        for c in ks[a]:
            c.wait_recv()
        for d in range(1, 8):
            total = total + kgr[a, (fi + d) % 8].astype(F32)
        kgs[a] = total.astype(BF16)
        kgall[a, own_rows] = kgs[a]
        return [send(kgs.at[a], kgall.at[a, own_rows], ch, f) for f in others]

    kq = [reduce_kernel(0)]
    back(0)
    kq.append(reduce_kernel(1))
    kq.append(reduce_kernel(2))

    s3.wait_recv()
    for half in range(2):
        p4[half] = (
            pbuf[here[0], half].astype(F32) + r2[0, 0, half].astype(F32)
            + r2[1, 0, half].astype(F32) + r3[half].astype(F32)
        ).astype(BF16)
    s4 = send(p4.at[oth], r4, sib)
    back(1)
    p_out[own] = p4[own]

    total = wgf[fi]
    for c in wq:
        c.wait_recv()
    for d in range(1, 8):
        total = total + wgq[(fi + d) % 8].astype(F32)
    wg_out[...] = total
    s4.wait_recv()
    p_out[oth] = r4[...]

    for a in range(3):
        for c in kq[a]:
            c.wait_recv()
        kg_out[9 * a : 9 * a + 9] = kgall[a].astype(F32).reshape(9, 128, 128)
    for c in sent:
        c.wait_send()


def body(inputs, conv_kernel, proj_weight, out_grad):
    x = inputs.transpose(1, 2, 0)
    o = out_grad.transpose(1, 0, 2)
    vmem = pl.BlockSpec(memory_space=pltpu.VMEM)
    shapes = [
        ((8, 2, 128, 1024), BF16),
        ((2, 1024, 128), BF16),
        ((4, 1088, 384), BF16),
        ((128, 3456), BF16),
        ((2, 2048, 128), BF16),
        ((256, 2048), BF16),
        ((2, 128, 1024), BF16),
        ((2, 128, 1024), BF16),
        ((2, 128, 1024), F32),
        ((8, 2, 128, 1024), BF16),
        ((2, 2, 128, 1024), BF16),
        ((2, 2, 2, 128, 1024), BF16),
        ((2, 128, 1024), BF16),
        ((2, 128, 1024), BF16),
        ((128, 1024), BF16),
        ((2, 128, 1024), F32),
        ((128, 1024), BF16),
        ((128, 1024), BF16),
        ((2, 128, 1024), BF16),
        ((2, 1024, 128), BF16),
        ((2, 1024, 128), BF16),
        ((4, 1088, 384), BF16),
        ((8, 256, 128), F32),
        ((8, 256, 128), BF16),
        ((8, 256, 128), BF16),
        ((8, 256, 128), BF16),
        ((8, 256, 128), BF16),
        ((3, 1152, 128), BF16),
        ((3, 8, 144, 128), BF16),
        ((3, 144, 128), BF16),
        ((3, 1152, 128), BF16),
    ]
    projected, input_grad, kernel_grad, weight_grad = pl.pallas_call(
        kernel,
        out_shape=(
            jax.ShapeDtypeStruct((2, 128, 1024), BF16),
            jax.ShapeDtypeStruct((2, 1024, 128), BF16),
            jax.ShapeDtypeStruct((27, 128, 128), F32),
            jax.ShapeDtypeStruct((256, 128), F32),
        ),
        in_specs=[vmem] * 4,
        out_specs=(vmem,) * 4,
        scratch_shapes=[pltpu.VMEM(s, d) for s, d in shapes]
        + [pltpu.SemaphoreType.DMA((N_SEMS,)), pltpu.SemaphoreType.DMA((N_SEMS,))],
        compiler_params=pltpu.CompilerParams(
            collective_id=0, has_side_effects=True, vmem_limit_bytes=56 * 1024 * 1024
        ),
    )(x, conv_kernel, proj_weight, o)
    return (
        projected.transpose(1, 0, 2), input_grad.transpose(2, 0, 1), kernel_grad, weight_grad
    )


def solution(mesh):
    in_specs = (
        P("chan", "filt", None),
        P(None, "chan", None),
        P("filt", "chan"),
        P("chan", "filt", None),
    )
    out_specs = (
        P("chan", "filt", None),
        P("chan", "filt", None),
        P(None, "chan", None),
        P("filt", "chan"),
    )
    return jax.shard_map(body, mesh=mesh, in_specs=in_specs, out_specs=out_specs, check_vma=False)
```

time: 481 us -> 129 us (0.27); the launches traced: 471 us -> 129 us
  waiting for transfers between devices: 277 us -> 0 us
  Pallas kernels: 0 us -> 118 us
  matrix products: 71.8 us -> 0 us
  blocking collectives: 44.4 us -> 0 us
  local copies, waits for them, and re-layouts: 46.7 us -> 10.3 us
  between operations: 15.6 us -> 0.65 us
  starting transfers between devices: 12.8 us -> 0 us
    unnamed x5 -> x0, waiting for transfers between devices: 140 us -> none
    pallas_call x0 -> x1, Pallas kernels: none -> 118 us  [body(): pl.pallas_call(kernel, out_shape=(jax.ShapeDtypeStruct((2, 128, 1024), BF...]
    dot_general x84 -> x0, matrix products: 71.8 us -> none  [the longest x27 36.5 us: body(): lax.dot_general(conv_grad, windows[tap], (((1,), (1,)), ((), ())), prefer...]
    reduce_scatter x1 -> x0, waiting for transfers between devices: 69.9 us -> none  [body(): lax.psum_scatter(weight_part.astype(jnp.bfloat16), 'filt', scatter_dimens...]
    psum x1 -> x0, waiting for transfers between devices: 61 us -> none  [body(): lax.psum(jnp.stack(kernel_parts, axis=0).astype(jnp.bfloat16), 'filt')]
    all_gather x1 -> x0, blocking collectives: 44.4 us -> none  [body(): w_cols = lax.all_gather(proj_weight, 'filt', axis=0, tiled=True)]
    convert_element_type x1 -> x0, local copies, waits for them, and re-layouts: 21.5 us -> none  [body(): projected = lax.psum_scatter(jnp.dot(portion, hidden, preferred_element_t...]
    ppermute x4 -> x0, starting transfers between devices: 12.4 us -> none  [the longest x2 9.84 us: with_halo(): before = lax.ppermute(last, axis, up)]
  transfers between devices with their start and end apart: 8 -> 0, of which waited for: 4 -> 0; matrix products, arithmetic and copies ran while one was open for 25% -> 0% of each run, Pallas kernels for 0% -> 0%
where the time goes in v1:
time: 129 us
  Pallas kernels  118 us (91%)
  local copies, waits for them, and re-layouts  10.3 us (8%)
    pallas_call x1, Pallas kernels, body(): pl.pallas_call(kernel, out_shape=(jax.ShapeDtypeStruct((2, 128, 1024), BF...  118 us
    unnamed x10, local copies, waits for them, and re-layouts  10.3 us

profile of v1, /device:TPU:0, one launch (start us, length us, event | category | flops | bytes accessed | tf_op | source)
XLA Modules:
  0.0 128.6 jit_solution(16005442379842489867)
XLA Ops:
  0.6 2.0 %copy.8 = bf16[128,2,1024]{0,2,1:T(8,128)(2,1)} copy(bf16[128,2,1024]{2,1,0:T(2,128)(2,1)} %param.4) | data formatting | bytes 1048576 | tf_op args[0]
  2.6 2.0 %copy.13 = bf16[128,2,1024]{2,0,1:T(8,128)(2,1)} copy(bf16[128,2,1024]{2,1,0:T(2,128)(2,1)} %param.7) | data formatting | bytes 1048576 | tf_op args[3]
  4.6 117.6 %shard_map.75 = (bf16[2,128,1024]{2,1,0:T(8,128)(2,1)}, bf16[2,1024,128]{2,1,0:T(8,128)(2,1)}, f32[27,128,128]{2,1,0:T(8,128)}, f32[256,128]{1,0:T(8,128)}) custom-call(bf16[2,1024,128]{2,1,0:T(8,128)(2,1)} %bitcast.6, bf16[27,128,128]{2,1,0:T(8,128)(2,1)} %k_ref.1, bf16[256,128]{1,0:T(8,128)(2,1)} %w_ref.1, bf16[2,128,1024]{2,1,0:T(8,128)(2,1)} %bitcast.7), custom_call_target="tpu_custom_call" | custom-call | tf_op jit(solution)/shard_map/pallas_call | solution.py:383
  122.2 0.0 copy-start
  122.2 2.5 %copy.10 = bf16[128,2,1024]{2,1,0:T(2,128)(2,1)} copy(bf16[128,2,1024]{2,0,1:T(8,128)(2,1)} %bitcast.9) | data formatting | bytes 1048576
  124.7 2.0 %copy.11 = bf16[128,2,1024]{2,1,0:T(2,128)(2,1)} copy(bf16[128,2,1024]{0,2,1:T(8,128)(2,1)} %bitcast.8) | data formatting | bytes 1048576
  126.7 0.0 copy-done
  126.7 0.0 copy-start.1
  126.7 1.2 copy.16
  127.9 0.0 copy-done.1
  127.9 0.7 copy.17
Async XLA Ops:
  122.2 4.5 %copy-start = (f32[27,128,128]{2,1,0:T(8,128)S(1)}, f32[27,128,128]{2,1,0:T(8,128)}, u32[]{:S(2)}) copy-start(f32[27,128,128]{2,1,0:T(8,128)} %get-tuple-element.22) | copy-start | bytes 5308420
  126.7 1.2 copy-start.1

commit v2 on v1

v2 whole, which is shorter than its diff:
```python
import jax
import jax.numpy as jnp
from jax import lax
from jax.experimental import pallas as pl
from jax.experimental.pallas import tpu as pltpu
from jax.sharding import PartitionSpec as P

MESH = pl.DeviceIdType.MESH
F32 = jnp.float32
BF16 = jnp.bfloat16
NN = (((1,), (0,)), ((), ()))
NT = (((1,), (1,)), ((), ()))
N_SEMS = 128


def dot(a, b, dims):
    return lax.dot_general(a, b, dims, preferred_element_type=F32)


def kernel(
    x_ref, k_ref, w_ref, o_ref,
    p_out, ig_out, kg_out, wg_out,
    obuf, xhalo, x3t, k3, wbuf, wt, hown, hbuf, der,
    pbuf, r1, r2, r3, p4, r4,
    ghb, ghs, ghr, cg, cgt, chalo, c3t, kback,
    wgf, wgs, wgr, wgp, wgq, wgy, wgz,
    kgf, kgb, kgr, kgs, kgy, kgall,
    ssem, rsem,
):
    ch = lax.axis_index("chan")
    fi = lax.axis_index("filt")
    co = ch % 2
    q = ch // 2
    yl = q % 2
    z = q // 2
    sib = ch + 1 - 2 * co
    zp = (ch + 4) % 16
    zm = (ch + 12) % 16
    yn = ch + 2 - 4 * yl
    own, oth = co, 1 - co
    flip = 1 - 2 * yl
    q_zp = ((z + 1) % 4) * 2 + yl
    q_zm = ((z + 3) % 4) * 2 + yl
    q_z2 = ((z + 2) % 4) * 2 + yl
    fx = fi // 2
    fy = fi + 1 - 2 * (fi % 2)
    f_up, f_dn = (fi + 1) % 8, (fi + 7) % 8
    fxs = [(fi + 2 * d) % 8 for d in range(1, 4)]
    sent = []

    def send(src, dst, chan_id, filt_id=None):
        i = len(sent)
        copy = pltpu.make_async_remote_copy(
            src_ref=src, dst_ref=dst, send_sem=ssem.at[i], recv_sem=rsem.at[i],
            device_id=(chan_id, fi if filt_id is None else filt_id), device_id_type=MESH,
        )
        copy.start()
        sent.append(copy)
        return copy

    def pass_on(ref, chan_id):
        return send(ref, ref, chan_id)

    barrier = pltpu.get_barrier_semaphore()
    for c in (sib, zp, zm, yn):
        pl.semaphore_signal(barrier, inc=1, device_id=(c, fi), device_id_type=MESH)
    for f in [f_up, f_dn] + fxs:
        pl.semaphore_signal(barrier, inc=1, device_id=(ch, f), device_id_type=MESH)
    pl.semaphore_wait(barrier, 9)

    c1 = send(o_ref.at[oth], obuf.at[q, own], sib)
    a_p = send(o_ref.at[own], obuf.at[q, own], zp)
    a_m = send(o_ref.at[own], obuf.at[q, own], zm)
    a_y = send(o_ref.at[own], obuf.at[q, own], yn)

    def block_of(f):
        return pl.ds(pl.multiple_of(f * 256, 256), 256)

    w_y = send(w_ref, wbuf.at[own, block_of(fi)], ch, fy)
    w_in = [send(w_ref, wbuf.at[own, block_of(fi)], ch, f) for f in fxs]

    wbuf[own, block_of(fi)] = w_ref[...]
    obuf[q, own] = o_ref[own]
    for t in range(27):
        a, lane = t // 9, (t % 9) * 128
        tap = k_ref[t]
        if a > 0:
            k3[0:128, (a - 1) * 1152 + lane : (a - 1) * 1152 + lane + 128] = tap
        if a < 2:
            k3[128:256, a * 1152 + lane : a * 1152 + lane + 128] = tap
        if a == 0:
            k3[0:128, 2304 + lane : 2304 + lane + 128] = tap
        if a == 2:
            k3[128:256, 2304 + lane : 2304 + lane + 128] = tap

    c1.wait_recv()
    b_y = pass_on(obuf.at[q, oth], yn)
    b_p = pass_on(obuf.at[q, oth], zp)
    b_m = pass_on(obuf.at[q, oth], zm)

    def spread(dst, at, src, low, keep):
        edge = jnp.zeros((32, 384), BF16)
        dst[at, 0:32] = edge
        dst[at, 1056:1088] = edge

        @pl.loop(0, 4)
        def _(i):
            rows = pl.ds(pl.multiple_of(i * 256, 256), 256)
            v = src[rows].astype(F32) * keep
            r = lax.broadcasted_iota(jnp.int32, (256, 128), 0) % 32
            prev = jnp.where(r == 0, 0.0, pltpu.roll(v, 1, 0))
            after = jnp.where(r == 31, 0.0, pltpu.roll(v, 255, 0))
            left, right = (prev, after) if low else (after, prev)
            to = pl.ds(pl.multiple_of(i * 256 + 32, 32), 256)
            dst[at, to, 0:128] = left.astype(BF16)
            dst[at, to, 128:256] = v.astype(BF16)
            dst[at, to, 256:384] = right.astype(BF16)

    one = jnp.float32(1.0)
    first = jnp.where(fi == 0, 0.0, 1.0).astype(F32)
    last = jnp.where(fi == 7, 0.0, 1.0).astype(F32)
    spread(x3t, 1, x_ref.at[0], True, one)
    spread(x3t, 2, x_ref.at[1], True, one)

    lower, upper = pl.ds(0, 64), pl.ds(64, 64)
    a_y.wait_recv()
    ya_p = pass_on(obuf.at[q + flip, own], zp)
    ya_m = pass_on(obuf.at[q + flip, own], zm)
    x_up = send(x_ref.at[1], xhalo.at[0], ch, f_up)
    x_dn = send(x_ref.at[0], xhalo.at[1], ch, f_dn)
    w_y.wait_recv()
    w_in += [
        send(wbuf.at[own, block_of(fy)], wbuf.at[own, block_of(fy)], ch, f) for f in fxs
    ]
    a_p.wait_recv()
    forwards = [pass_on(obuf.at[q_zm, own, lower], zp)]
    a_m.wait_recv()
    forwards.append(pass_on(obuf.at[q_zp, own, upper], zm))

    def windows(src, plane, i, order):
        return [
            src[plane, pl.ds(pl.multiple_of(i * 256 + 32 * b, 32), 256)] for b in order
        ]

    def convolve(start, stop):
        @pl.loop(start, stop)
        def _(i):
            cols = pl.ds(pl.multiple_of(i * 256, 256), 256)
            wins = windows(x3t, 1, i, range(3)) + windows(x3t, 2, i, range(3))
            v = dot(k3[:, 0:2304], jnp.concatenate(wins, axis=1), NT)
            der[0, :, cols] = v[:128]
            der[1, :, cols] = v[128:]

    def activate(plane):
        @pl.loop(0, 4)
        def _(i):
            cols = pl.ds(pl.multiple_of(i * 256, 256), 256)
            wins = windows(x3t, 3 * plane, i, range(3))
            taps = k3[pl.ds(pl.multiple_of(plane * 128, 128), 128), 2304:3456]
            v = der[plane, :, cols] + dot(taps, jnp.concatenate(wins, axis=1), NT)
            s = 0.7978845608028654
            sq = v * v
            t = jnp.tanh(s * (v + 0.044715 * sq * v))
            hown[plane, :, cols] = (0.5 * v * (1.0 + t)).astype(BF16)
            der[plane, :, cols] = 0.5 * (1.0 + t) + 0.5 * v * (1.0 - t * t) * (
                s * (1.0 + 3 * 0.044715 * sq)
            )

    convolve(0, 2)
    b_y.wait_recv()
    yb_p = pass_on(obuf.at[q + flip, oth], zp)
    yb_m = pass_on(obuf.at[q + flip, oth], zm)
    b_p.wait_recv()
    forwards.append(pass_on(obuf.at[q_zm, oth, lower], zp))
    b_m.wait_recv()
    forwards.append(pass_on(obuf.at[q_zp, oth, upper], zm))
    convolve(2, 4)
    for c in w_in:
        c.wait_recv()
    w_sib = send(wbuf.at[own], wbuf.at[own], sib)

    x_up.wait_recv()
    x_dn.wait_recv()
    spread(x3t, 0, xhalo.at[0], True, first)
    spread(x3t, 3, xhalo.at[1], True, last)
    activate(oth)
    h_x = send(hown.at[oth], hbuf.at[own], sib)
    ya_p.wait_recv()
    forwards.append(pass_on(obuf.at[q_zm + flip, own, lower], zp))
    ya_m.wait_recv()
    forwards.append(pass_on(obuf.at[q_zp + flip, own, upper], zm))
    activate(own)
    hbuf[own] = hown[own]

    w_sib.wait_recv()

    @pl.loop(0, 8)
    def _(j):
        rows = block_of(j)
        for half in range(2):
            block = wbuf[half, rows].astype(F32)
            wt[half * 128 : (half + 1) * 128, rows] = block.T.astype(BF16)

    yb_p.wait_recv()
    forwards.append(pass_on(obuf.at[q_zm + flip, oth, lower], zp))
    yb_m.wait_recv()
    forwards.append(pass_on(obuf.at[q_zp + flip, oth, upper], zm))
    h_x.wait_recv()

    def project(at):
        rows = block_of(at)
        w = jnp.concatenate([wbuf[0, rows], wbuf[1, rows]], axis=1)

        @pl.loop(0, 4)
        def _(i):
            cols = pl.ds(pl.multiple_of(i * 256, 256), 256)
            h = jnp.concatenate([hbuf[0, :, cols], hbuf[1, :, cols]], axis=0)
            v = dot(w, h, NN).astype(BF16)
            pbuf[at, 0, :, cols] = v[:128]
            pbuf[at, 1, :, cols] = v[128:]

    far = (q_z2 + flip, q_z2)
    up = (q_zp + flip, q_zp)
    down = (q_zm + flip, q_zm)
    here = (q + flip, q)
    for at in far + up + down + here:
        project(at)

    for c in forwards:
        c.wait_recv()
    s1 = [
        (send(pbuf.at[far[i], 0], r1.at[0, i], zp), send(pbuf.at[far[i], 1], r1.at[1, i], zm))
        for i in range(2)
    ]

    @pl.loop(0, 4)
    def _(i):
        cols = pl.ds(pl.multiple_of(i * 256, 256), 256)
        o = obuf[:, :, :, cols].reshape(2048, 256)
        v = dot(wt[...], o, NN)
        ghb[0, :, cols] = v[:128]
        ghb[1, :, cols] = v[128:]

    ghs[...] = ghb[oth].astype(BF16)
    g_x = send(ghs, ghr, sib)

    def to_grad(plane, source):
        @pl.loop(0, 4)
        def _(i):
            cols = pl.ds(pl.multiple_of(i * 256, 256), 256)
            v = (source[:, cols].astype(F32) * der[plane, :, cols]).astype(BF16)
            cg[plane, :, cols] = v
            cgt[plane, cols] = v.astype(F32).T.astype(BF16)

    to_grad(own, ghb.at[own])
    g_x.wait_recv()
    to_grad(oth, ghr)
    g_up = send(cgt.at[1], chalo.at[0], ch, f_up)
    g_dn = send(cgt.at[0], chalo.at[1], ch, f_dn)

    def second(i):
        for side, block in ((0, up[i]), (1, down[i])):
            s1[i][side].wait_recv()
            pbuf[block, side] = (
                pbuf[block, side].astype(F32) + r1[side, i].astype(F32)
            ).astype(BF16)
        return (
            send(pbuf.at[up[i]], r2.at[0, i], zp), send(pbuf.at[down[i]], r2.at[1, i], zm)
        )

    s2 = [second(0)]

    def window_row(plane):
        return jnp.concatenate([x3t[plane, 32 * b : 32 * b + 1024] for b in range(3)], axis=1)

    both = cg[...].reshape(256, 1024)

    def x_slice(f):
        return pl.ds(pl.multiple_of((f // 2) * 288, 32), 288)

    def kernel_chunk(a, value):
        for t in range(9):
            kgb[a, t * 128 : (t + 1) * 128] = value[:, t * 128 : (t + 1) * 128].astype(BF16)
        return [send(kgb.at[a, x_slice(f)], kgr.at[a, fx], ch, f) for f in fxs]

    kgf[...] = dot(both, window_row(1), NN)
    ks = [kernel_chunk(0, kgf[128:] + dot(cg[0], window_row(0), NN))]
    s2.append(second(1))
    v2 = dot(both, window_row(2), NN)
    ks.append(kernel_chunk(1, kgf[:128] + v2[128:]))
    ks.append(kernel_chunk(2, v2[:128] + dot(cg[1], window_row(3), NN)))

    @pl.loop(0, 8)
    def _(j):
        h = jnp.concatenate([hbuf[0], hbuf[1]], axis=0)
        v = dot(obuf[j].reshape(256, 1024), h, NT)
        lo, hi = v[:, :128], v[:, 128:]
        wgf[j] = jnp.where(co == 0, lo, hi)
        wgs[j] = jnp.where(co == 0, hi, lo).astype(BF16)

    wg_x = send(wgs, wgr, sib)

    def kernel_pair(a):
        total = kgb[a, x_slice(fi)].astype(F32)
        for c in ks[a]:
            c.wait_recv()
        for f in fxs:
            total = total + kgr[a, f // 2].astype(F32)
        kgs[a] = total.astype(BF16)
        return send(kgs.at[a], kgy.at[a], ch, fy)

    ky = [kernel_pair(0)]
    spread(c3t, 1, cgt.at[0], False, one)
    spread(c3t, 2, cgt.at[1], False, one)

    for j, (a0, a1) in enumerate(((1, 2), (0, 1))):
        rows = slice(j * 1152, (j + 1) * 1152)
        kback[rows, 0:128] = k_ref[9 * a0 : 9 * a0 + 9].reshape(1152, 128)
        kback[rows, 128:256] = k_ref[9 * a1 : 9 * a1 + 9].reshape(1152, 128)
    back = (2, 1, 0)

    @pl.loop(0, 4)
    def _(i):
        cols = pl.ds(pl.multiple_of(i * 256, 256), 256)
        wins = windows(c3t, 1, i, back) + windows(c3t, 2, i, back)
        v = dot(jnp.concatenate(wins, axis=1), kback[...], NN)
        ghb[0, :, cols] = v[:, :128].T
        ghb[1, :, cols] = v[:, 128:].T

    ky.append(kernel_pair(1))
    ky.append(kernel_pair(2))
    wg_x.wait_recv()
    wgf[...] = wgf[...] + wgr[...].astype(F32)
    wgp[...] = wgf[...].astype(BF16)

    def f_pair(f):
        return pl.ds((f // 2) * 2, 2)

    wq = [send(wgp.at[f_pair(f)], wgq.at[fx], ch, f) for f in fxs]

    for c in s2[0]:
        c.wait_recv()
    pbuf[here[0]] = (
        pbuf[here[0]].astype(F32) + r2[0, 0].astype(F32) + r2[1, 0].astype(F32)
    ).astype(BF16)
    s3 = send(pbuf.at[here[0]], r3, yn)

    kq = []
    for a in range(3):
        ky[a].wait_recv()
        kgall[a, x_slice(fi)] = (kgs[a].astype(F32) + kgy[a].astype(F32)).astype(BF16)
        kq += [
            send(kgall.at[a, x_slice(fi)], kgall.at[a, x_slice(fi)], ch, f) for f in fxs
        ]

    g_up.wait_recv()
    g_dn.wait_recv()
    spread(c3t, 0, chalo.at[0], False, first)
    spread(c3t, 3, chalo.at[1], False, last)

    for plane in range(2):
        @pl.loop(0, 4)
        def _(i):
            cols = pl.ds(pl.multiple_of(i * 256, 256), 256)
            wins = windows(c3t, 3 * plane, i, back)
            taps = k_ref[18 * (1 - plane) : 18 * (1 - plane) + 9].reshape(1152, 128)
            v = dot(jnp.concatenate(wins, axis=1), taps, NN)
            ig_out[plane, :, cols] = (ghb[plane, :, cols] + v.T).astype(BF16)

    total = wgf[f_pair(fi)]
    for c in wq:
        c.wait_recv()
    for f in fxs:
        total = total + wgq[f // 2].astype(F32)
    wgf[f_pair(fi)] = total
    wgy[...] = wgf[fy].astype(BF16)
    wy = send(wgy, wgz, ch, fy)

    for c in s2[1]:
        c.wait_recv()
    s3.wait_recv()
    for half in range(2):
        p4[half] = (
            pbuf[here[1], half].astype(F32) + r2[0, 1, half].astype(F32)
            + r2[1, 1, half].astype(F32) + r3[half].astype(F32)
        ).astype(BF16)
    s4 = send(p4.at[oth], r4, sib)
    p_out[own] = p4[own]
    wy.wait_recv()
    wg_out[...] = wgf[fi] + wgz[...].astype(F32)
    for c in kq:
        c.wait_recv()
    for a in range(3):
        kg_out[9 * a : 9 * a + 9] = kgall[a].astype(F32).reshape(9, 128, 128)
    s4.wait_recv()
    p_out[oth] = r4[...]
    for c in sent:
        c.wait_send()


def body(inputs, conv_kernel, proj_weight, out_grad):
    x = inputs.transpose(1, 2, 0)
    o = out_grad.transpose(1, 0, 2)
    vmem = pl.BlockSpec(memory_space=pltpu.VMEM)
    shapes = [
        ((8, 2, 128, 1024), BF16),
        ((2, 1024, 128), BF16),
        ((4, 1088, 384), BF16),
        ((256, 3456), BF16),
        ((2, 2048, 128), BF16),
        ((256, 2048), BF16),
        ((2, 128, 1024), BF16),
        ((2, 128, 1024), BF16),
        ((2, 128, 1024), F32),
        ((8, 2, 128, 1024), BF16),
        ((2, 2, 128, 1024), BF16),
        ((2, 2, 2, 128, 1024), BF16),
        ((2, 128, 1024), BF16),
        ((2, 128, 1024), BF16),
        ((128, 1024), BF16),
        ((2, 128, 1024), F32),
        ((128, 1024), BF16),
        ((128, 1024), BF16),
        ((2, 128, 1024), BF16),
        ((2, 1024, 128), BF16),
        ((2, 1024, 128), BF16),
        ((4, 1088, 384), BF16),
        ((2304, 256), BF16),
        ((8, 256, 128), F32),
        ((8, 256, 128), BF16),
        ((8, 256, 128), BF16),
        ((8, 256, 128), BF16),
        ((4, 2, 256, 128), BF16),
        ((256, 128), BF16),
        ((256, 128), BF16),
        ((256, 1152), F32),
        ((3, 1152, 128), BF16),
        ((3, 4, 288, 128), BF16),
        ((3, 288, 128), BF16),
        ((3, 288, 128), BF16),
        ((3, 1152, 128), BF16),
    ]
    projected, input_grad, kernel_grad, weight_grad = pl.pallas_call(
        kernel,
        out_shape=(
            jax.ShapeDtypeStruct((2, 128, 1024), BF16),
            jax.ShapeDtypeStruct((2, 128, 1024), BF16),
            jax.ShapeDtypeStruct((27, 128, 128), F32),
            jax.ShapeDtypeStruct((256, 128), F32),
        ),
        in_specs=[vmem] * 4,
        out_specs=(vmem,) * 4,
        scratch_shapes=[pltpu.VMEM(s, d) for s, d in shapes]
        + [pltpu.SemaphoreType.DMA((N_SEMS,)), pltpu.SemaphoreType.DMA((N_SEMS,))],
        compiler_params=pltpu.CompilerParams(
            collective_id=0, has_side_effects=True, vmem_limit_bytes=56 * 1024 * 1024
        ),
    )(x, conv_kernel, proj_weight, o)
    return (
        projected.transpose(1, 0, 2), input_grad.transpose(1, 0, 2), kernel_grad, weight_grad
    )


def solution(mesh):
    in_specs = (
        P("chan", "filt", None),
        P(None, "chan", None),
        P("filt", "chan"),
        P("chan", "filt", None),
    )
    out_specs = (
        P("chan", "filt", None),
        P("chan", "filt", None),
        P(None, "chan", None),
        P("filt", "chan"),
    )
    return jax.shard_map(body, mesh=mesh, in_specs=in_specs, out_specs=out_specs, check_vma=False)
```

time: 129 us -> 101 us (0.78)
  Pallas kernels: 118 us -> 89.7 us
    pallas_call x1, Pallas kernels: 118 us -> 89.7 us  [body(): pl.pallas_call(kernel, out_shape=(jax.ShapeDtypeStruct((2, 128, 1024), BF...]
where the time goes in v2:
time: 101 us
  Pallas kernels  89.7 us (89%)
  local copies, waits for them, and re-layouts  10.7 us (11%)
    pallas_call x1, Pallas kernels, body(): pl.pallas_call(kernel, out_shape=(jax.ShapeDtypeStruct((2, 128, 1024), BF...  89.7 us
    unnamed x10, local copies, waits for them, and re-layouts  10.7 us

profile of v2, /device:TPU:0, one launch (start us, length us, event | category | flops | bytes accessed | tf_op | source)
XLA Modules:
  0.0 101.0 jit_solution(16979290402887557167)
XLA Ops:
  0.6 2.0 %copy.8 = bf16[128,2,1024]{0,2,1:T(8,128)(2,1)} copy(bf16[128,2,1024]{2,1,0:T(2,128)(2,1)} %param.4) | data formatting | bytes 1048576 | tf_op args[0]
  2.6 2.0 %copy.13 = bf16[128,2,1024]{2,0,1:T(8,128)(2,1)} copy(bf16[128,2,1024]{2,1,0:T(2,128)(2,1)} %param.7) | data formatting | bytes 1048576 | tf_op args[3]
  4.6 89.7 %shard_map.75 = (bf16[2,128,1024]{2,1,0:T(8,128)(2,1)}, bf16[2,128,1024]{2,1,0:T(8,128)(2,1)}, f32[27,128,128]{2,1,0:T(8,128)}, f32[256,128]{1,0:T(8,128)}) custom-call(bf16[2,1024,128]{2,1,0:T(8,128)(2,1)} %bitcast.6, bf16[27,128,128]{2,1,0:T(8,128)(2,1)} %k_ref.1, bf16[256,128]{1,0:T(8,128)(2,1)} %w_ref.1, bf16[2,128,1024]{2,1,0:T(8,128)(2,1)} %bitcast.7), custom_call_target="tpu_custom_call" | custom-call | tf_op jit(solution)/shard_map/pallas_call | solution.py:443
  94.3 0.0 copy-start
  94.3 2.5 %copy.10 = bf16[128,2,1024]{2,1,0:T(2,128)(2,1)} copy(bf16[128,2,1024]{2,0,1:T(8,128)(2,1)} %bitcast.9) | data formatting | bytes 1048576
  96.8 2.4 %copy.11 = bf16[128,2,1024]{2,1,0:T(2,128)(2,1)} copy(bf16[128,2,1024]{2,0,1:T(8,128)(2,1)} %bitcast.8) | data formatting | bytes 1048576
  99.2 0.0 copy-done
  99.2 0.0 copy-start.1
  99.2 1.2 %copy.16 = f32[27,128,128]{2,1,0:T(8,128)} copy(f32[27,128,128]{2,1,0:T(8,128)S(1)} %copy-done) | data formatting | bytes 3538944
  100.4 0.0 copy-done.1
  100.4 0.7 copy.17
Async XLA Ops:
  94.3 4.9 %copy-start = (f32[27,128,128]{2,1,0:T(8,128)S(1)}, f32[27,128,128]{2,1,0:T(8,128)}, u32[]{:S(2)}) copy-start(f32[27,128,128]{2,1,0:T(8,128)} %get-tuple-element.22) | copy-start | bytes 5308420
  99.2 1.2 %copy-start.1 = (f32[256,128]{1,0:T(8,128)S(1)}, f32[256,128]{1,0:T(8,128)}, u32[]{:S(2)}) copy-start(f32[256,128]{1,0:T(8,128)} %get-tuple-element.23) | copy-start | bytes 393220

commit v3 on v2

--- a/solution.py
+++ b/solution.py
@@ -18,14 +18,16 @@
 
 
 def kernel(
-    x_ref, k_ref, w_ref, o_ref,
+    x_in, k_in, w_in_ref, o_in,
+    p_res, ig_res, kg_res, wg_res,
+    x_raw, k_ref, w_ref, o_raw, x_ref, o_ref,
     p_out, ig_out, kg_out, wg_out,
     obuf, xhalo, x3t, k3, wbuf, wt, hown, hbuf, der,
-    pbuf, r1, r2, r3, p4, r4,
+    pbuf, sbuf, r1, r2, r3,
     ghb, ghs, ghr, cg, cgt, chalo, c3t, kback,
     wgf, wgs, wgr, wgp, wgq, wgy, wgz,
     kgf, kgb, kgr, kgs, kgy, kgall,
-    ssem, rsem,
+    ssem, rsem, lsem,
 ):
     ch = lax.axis_index("chan")
     fi = lax.axis_index("filt")
@@ -61,11 +63,25 @@
     def pass_on(ref, chan_id):
         return send(ref, ref, chan_id)
 
+    def local(src, dst, i):
+        copy = pltpu.make_async_copy(src, dst, lsem.at[i])
+        copy.start()
+        return copy
+
+    o_load = local(o_in, o_raw, 0)
+    w_load = local(w_in_ref, w_ref, 1)
+    x_load = local(x_in, x_raw, 2)
+    k_load = local(k_in, k_ref, 3)
+
     barrier = pltpu.get_barrier_semaphore()
     for c in (sib, zp, zm, yn):
         pl.semaphore_signal(barrier, inc=1, device_id=(c, fi), device_id_type=MESH)
     for f in [f_up, f_dn] + fxs:
         pl.semaphore_signal(barrier, inc=1, device_id=(ch, f), device_id_type=MESH)
+    o_load.wait()
+    for plane in range(2):
+        o_ref[plane] = o_raw[:, plane]
+    w_load.wait()
     pl.semaphore_wait(barrier, 9)
 
     c1 = send(o_ref.at[oth], obuf.at[q, own], sib)
@@ -81,6 +97,19 @@
 
     wbuf[own, block_of(fi)] = w_ref[...]
     obuf[q, own] = o_ref[own]
+    x_load.wait()
+    for plane in range(2):
+        @pl.loop(0, 4)
+        def _(i):
+            cols = pl.ds(pl.multiple_of(i * 256, 256), 256)
+            x_ref[plane, cols] = x_raw[:, plane, cols].astype(F32).T.astype(BF16)
+
+    c1.wait_recv()
+    b_y = pass_on(obuf.at[q, oth], yn)
+    b_p = pass_on(obuf.at[q, oth], zp)
+    b_m = pass_on(obuf.at[q, oth], zm)
+
+    k_load.wait()
     for t in range(27):
         a, lane = t // 9, (t % 9) * 128
         tap = k_ref[t]
@@ -93,11 +122,6 @@
         if a == 2:
             k3[128:256, 2304 + lane : 2304 + lane + 128] = tap
 
-    c1.wait_recv()
-    b_y = pass_on(obuf.at[q, oth], yn)
-    b_p = pass_on(obuf.at[q, oth], zp)
-    b_m = pass_on(obuf.at[q, oth], zm)
-
     def spread(dst, at, src, low, keep):
         edge = jnp.zeros((32, 384), BF16)
         dst[at, 0:32] = edge
@@ -124,8 +148,8 @@
 
     lower, upper = pl.ds(0, 64), pl.ds(64, 64)
     a_y.wait_recv()
-    ya_p = pass_on(obuf.at[q + flip, own], zp)
-    ya_m = pass_on(obuf.at[q + flip, own], zm)
+    ya_p = pass_on(obuf.at[q + flip, own, upper], zp)
+    ya_m = pass_on(obuf.at[q + flip, own, upper], zm)
     x_up = send(x_ref.at[1], xhalo.at[0], ch, f_up)
     x_dn = send(x_ref.at[0], xhalo.at[1], ch, f_dn)
     w_y.wait_recv()
@@ -134,8 +158,10 @@
     ]
     a_p.wait_recv()
     forwards = [pass_on(obuf.at[q_zm, own, lower], zp)]
+    across = [pass_on(obuf.at[q_zm, own, lower], yn)]
     a_m.wait_recv()
     forwards.append(pass_on(obuf.at[q_zp, own, upper], zm))
+    across.append(pass_on(obuf.at[q_zp, own, lower], yn))
 
     def windows(src, plane, i, order):
         return [
@@ -175,6 +201,8 @@
     b_m.wait_recv()
     forwards.append(pass_on(obuf.at[q_zp, oth, upper], zm))
     convolve(2, 4)
+    forwards[0].wait_recv()
+    across.append(pass_on(obuf.at[q_z2, own, lower], yn))
     for c in w_in:
         c.wait_recv()
     w_sib = send(wbuf.at[own], wbuf.at[own], sib)
@@ -186,9 +214,9 @@
     activate(oth)
     h_x = send(hown.at[oth], hbuf.at[own], sib)
     ya_p.wait_recv()
-    forwards.append(pass_on(obuf.at[q_zm + flip, own, lower], zp))
+    forwards.append(pass_on(obuf.at[q_zm + flip, own, pl.ds(64, 32)], zp))
     ya_m.wait_recv()
-    forwards.append(pass_on(obuf.at[q_zp + flip, own, upper], zm))
+    forwards.append(pass_on(obuf.at[q_zp + flip, own, pl.ds(96, 32)], zm))
     activate(own)
     hbuf[own] = hown[own]
 
@@ -215,23 +243,28 @@
         def _(i):
             cols = pl.ds(pl.multiple_of(i * 256, 256), 256)
             h = jnp.concatenate([hbuf[0, :, cols], hbuf[1, :, cols]], axis=0)
-            v = dot(w, h, NN).astype(BF16)
-            pbuf[at, 0, :, cols] = v[:128]
-            pbuf[at, 1, :, cols] = v[128:]
+            v = dot(w, h, NN)
+            lo, hi = v[:128], v[128:]
+            pbuf[at, own, :, cols] = jnp.where(co == 0, lo, hi).astype(BF16)
+            sbuf[at, :, cols] = jnp.where(co == 0, hi, lo).astype(BF16)
+
+        return send(sbuf.at[at], pbuf.at[at, own], sib)
 
     far = (q_z2 + flip, q_z2)
     up = (q_zp + flip, q_zp)
     down = (q_zm + flip, q_zm)
     here = (q + flip, q)
-    for at in far + up + down + here:
-        project(at)
-
-    for c in forwards:
+    ph_far = [project(at) for at in far]
+    ph_near = [project(up[0]), project(down[0])]
+    s1 = []
+    for i in range(2):
+        ph_far[i].wait_recv()
+        s1.append((
+            send(pbuf.at[far[i], 0], r1.at[0, i], zp), send(pbuf.at[far[i], 1], r1.at[1, i], zm)
+        ))
+    ph_near += [project(at) for at in (up[1], down[1]) + here]
+    for c in forwards[1:] + across:
         c.wait_recv()
-    s1 = [
-        (send(pbuf.at[far[i], 0], r1.at[0, i], zp), send(pbuf.at[far[i], 1], r1.at[1, i], zm))
-        for i in range(2)
-    ]
 
     @pl.loop(0, 4)
     def _(i):
@@ -257,6 +290,9 @@
     to_grad(oth, ghr)
     g_up = send(cgt.at[1], chalo.at[0], ch, f_up)
     g_dn = send(cgt.at[0], chalo.at[1], ch, f_dn)
+
+    for c in ph_near:
+        c.wait_recv()
 
     def second(i):
         for side, block in ((0, up[i]), (1, down[i])):
@@ -285,7 +321,6 @@
 
     kgf[...] = dot(both, window_row(1), NN)
     ks = [kernel_chunk(0, kgf[128:] + dot(cg[0], window_row(0), NN))]
-    s2.append(second(1))
     v2 = dot(both, window_row(2), NN)
     ks.append(kernel_chunk(1, kgf[:128] + v2[128:]))
     ks.append(kernel_chunk(2, v2[:128] + dot(cg[1], window_row(3), NN)))
@@ -344,6 +379,7 @@
         pbuf[here[0]].astype(F32) + r2[0, 0].astype(F32) + r2[1, 0].astype(F32)
     ).astype(BF16)
     s3 = send(pbuf.at[here[0]], r3, yn)
+    s2.append(second(1))
 
     kq = []
     for a in range(3):
@@ -365,8 +401,9 @@
             wins = windows(c3t, 3 * plane, i, back)
             taps = k_ref[18 * (1 - plane) : 18 * (1 - plane) + 9].reshape(1152, 128)
             v = dot(jnp.concatenate(wins, axis=1), taps, NN)
-            ig_out[plane, :, cols] = (ghb[plane, :, cols] + v.T).astype(BF16)
-
+            ig_out[:, plane, cols] = (ghb[plane, :, cols] + v.T).astype(BF16)
+
+    ig_store = local(ig_out, ig_res, 4)
     total = wgf[f_pair(fi)]
     for c in wq:
         c.wait_recv()
@@ -376,33 +413,43 @@
     wgy[...] = wgf[fy].astype(BF16)
     wy = send(wgy, wgz, ch, fy)
 
+    wy.wait_recv()
+    wg_out[...] = wgf[fi] + wgz[...].astype(F32)
+    stores = [ig_store, local(wg_out, wg_res, 5)]
+    for a in range(3):
+        for c in kq[3 * a : 3 * a + 3]:
+            c.wait_recv()
+        kg_out[9 * a : 9 * a + 9] = kgall[a].astype(F32).reshape(9, 128, 128)
+        part = pl.ds(9 * a, 9)
+        stores.append(local(kg_out.at[part], kg_res.at[part], 6 + a))
     for c in s2[1]:
         c.wait_recv()
     s3.wait_recv()
-    for half in range(2):
-        p4[half] = (
-            pbuf[here[1], half].astype(F32) + r2[0, 1, half].astype(F32)
-            + r2[1, 1, half].astype(F32) + r3[half].astype(F32)
+    for plane in range(2):
+        p_out[:, plane] = (
+            pbuf[here[1], plane].astype(F32) + r2[0, 1, plane].astype(F32)
+            + r2[1, 1, plane].astype(F32) + r3[plane].astype(F32)
         ).astype(BF16)
-    s4 = send(p4.at[oth], r4, sib)
-    p_out[own] = p4[own]
-    wy.wait_recv()
-    wg_out[...] = wgf[fi] + wgz[...].astype(F32)
-    for c in kq:
-        c.wait_recv()
-    for a in range(3):
-        kg_out[9 * a : 9 * a + 9] = kgall[a].astype(F32).reshape(9, 128, 128)
-    s4.wait_recv()
-    p_out[oth] = r4[...]
+    stores.append(local(p_out, p_res, 9))
+    for c in stores:
+        c.wait()
     for c in sent:
         c.wait_send()
 
 
 def body(inputs, conv_kernel, proj_weight, out_grad):
-    x = inputs.transpose(1, 2, 0)
-    o = out_grad.transpose(1, 0, 2)
-    vmem = pl.BlockSpec(memory_space=pltpu.VMEM)
+    anywhere = pl.BlockSpec(memory_space=pl.ANY)
     shapes = [
+        ((128, 2, 1024), BF16),
+        ((27, 128, 128), BF16),
+        ((256, 128), BF16),
+        ((128, 2, 1024), BF16),
+        ((2, 1024, 128), BF16),
+        ((2, 128, 1024), BF16),
+        ((128, 2, 1024), BF16),
+        ((128, 2, 1024), BF16),
+        ((27, 128, 128), F32),
+        ((256, 128), F32),
         ((8, 2, 128, 1024), BF16),
         ((2, 1024, 128), BF16),
         ((4, 1088, 384), BF16),
@@ -413,11 +460,10 @@
         ((2, 128, 1024), BF16),
         ((2, 128, 1024), F32),
         ((8, 2, 128, 1024), BF16),
+        ((8, 128, 1024), BF16),
         ((2, 2, 128, 1024), BF16),
         ((2, 2, 2, 128, 1024), BF16),
         ((2, 128, 1024), BF16),
-        ((2, 128, 1024), BF16),
-        ((128, 1024), BF16),
         ((2, 128, 1024), F32),
         ((128, 1024), BF16),
         ((128, 1024), BF16),
@@ -440,25 +486,22 @@
         ((3, 288, 128), BF16),
         ((3, 1152, 128), BF16),
     ]
-    projected, input_grad, kernel_grad, weight_grad = pl.pallas_call(
+    return pl.pallas_call(
         kernel,
         out_shape=(
-            jax.ShapeDtypeStruct((2, 128, 1024), BF16),
-            jax.ShapeDtypeStruct((2, 128, 1024), BF16),
+            jax.ShapeDtypeStruct((128, 2, 1024), BF16),
+            jax.ShapeDtypeStruct((128, 2, 1024), BF16),
             jax.ShapeDtypeStruct((27, 128, 128), F32),
             jax.ShapeDtypeStruct((256, 128), F32),
         ),
-        in_specs=[vmem] * 4,
-        out_specs=(vmem,) * 4,
+        in_specs=[anywhere] * 4,
+        out_specs=(anywhere,) * 4,
         scratch_shapes=[pltpu.VMEM(s, d) for s, d in shapes]
-        + [pltpu.SemaphoreType.DMA((N_SEMS,)), pltpu.SemaphoreType.DMA((N_SEMS,))],
+        + [pltpu.SemaphoreType.DMA((N_SEMS,)), pltpu.SemaphoreType.DMA((N_SEMS,)), pltpu.SemaphoreType.DMA((10,))],
         compiler_params=pltpu.CompilerParams(
             collective_id=0, has_side_effects=True, vmem_limit_bytes=56 * 1024 * 1024
         ),
-    )(x, conv_kernel, proj_weight, o)
-    return (
-        projected.transpose(1, 0, 2), input_grad.transpose(1, 0, 2), kernel_grad, weight_grad
-    )
+    )(inputs, conv_kernel, proj_weight, out_grad)
 
 
 def solution(mesh):

time: 101 us -> 95.9 us (0.950)
  local copies, waits for them, and re-layouts: 10.7 us -> 6.39 us
  Pallas kernels: 89.7 us -> 88.3 us
    unnamed x10 -> x8, local copies, waits for them, and re-layouts: 10.7 us -> 6.39 us
    pallas_call x1, Pallas kernels: 89.7 us -> 88.3 us  [body(): pl.pallas_call(kernel, out_shape=(jax.ShapeDtypeStruct((128, 2, 1024), BF...]
where the time goes in v3:
time: 95.9 us; the launch traced here: 95.3 us
  Pallas kernels  88.3 us (92%)
  local copies, waits for them, and re-layouts  6.39 us (7%)
    pallas_call x1, Pallas kernels, body(): pl.pallas_call(kernel, out_shape=(jax.ShapeDtypeStruct((128, 2, 1024), BF...  88.3 us
    unnamed x8, local copies, waits for them, and re-layouts  6.39 us

profile of v3, /device:TPU:0, one launch (start us, length us, event | category | flops | bytes accessed | tf_op | source)
XLA Modules:
  0.0 95.3 jit_solution(17522469932982807267)
XLA Ops:
  0.6 88.3 %shard_map.75 = (bf16[128,2,1024]{2,1,0:T(2,128)(2,1)}, bf16[128,2,1024]{2,1,0:T(2,128)(2,1)}, f32[27,128,128]{2,1,0:T(8,128)}, f32[256,128]{1,0:T(8,128)}) custom-call(bf16[128,2,1024]{2,1,0:T(2,128)(2,1)} %x_in.1, bf16[27,128,128]{2,1,0:T(8,128)(2,1)} %k_in.1, bf16[256,128]{1,0:T(8,128)(2,1)} %w_in_ref.1, bf16[128,2,1024]{2,1,0:T(2,128)(2,1)} %o_in.1), custom_call_target="tpu_custom_call" | custom-call | tf_op jit(solution)/shard_map/pallas_call | solution.py:489
  88.9 0.0 copy-start
  88.9 2.3 %copy.12 = bf16[128,2,1024]{2,1,0:T(2,128)(2,1)} copy(bf16[128,2,1024]{2,1,0:T(2,128)(2,1)} %get-tuple-element.8) | data formatting | bytes 1048576
  91.3 2.2 %copy.13 = bf16[128,2,1024]{2,1,0:T(2,128)(2,1)} copy(bf16[128,2,1024]{2,1,0:T(2,128)(2,1)} %get-tuple-element.9) | data formatting | bytes 1048576
  93.5 0.0 copy-done
  93.5 0.0 copy-start.1
  93.5 1.2 %copy.14 = f32[27,128,128]{2,1,0:T(8,128)} copy(f32[27,128,128]{2,1,0:T(8,128)S(1)} %copy-done) | data formatting | bytes 3538944
  94.7 0.0 copy-done.1
  94.7 0.7 copy.15
Async XLA Ops:
  88.9 4.5 %copy-start = (f32[27,128,128]{2,1,0:T(8,128)S(1)}, f32[27,128,128]{2,1,0:T(8,128)}, u32[]{:S(2)}) copy-start(f32[27,128,128]{2,1,0:T(8,128)} %get-tuple-element.10) | copy-start | bytes 5308420
  93.5 1.2 %copy-start.1 = (f32[256,128]{1,0:T(8,128)S(1)}, f32[256,128]{1,0:T(8,128)}, u32[]{:S(2)}) copy-start(f32[256,128]{1,0:T(8,128)} %get-tuple-element.11) | copy-start | bytes 393220

commit v4 on v3

--- a/solution.py
+++ b/solution.py
@@ -11,6 +11,7 @@
 NN = (((1,), (0,)), ((), ()))
 NT = (((1,), (1,)), ((), ()))
 N_SEMS = 128
+PIECES = (2, 2, 3, 1)
 
 
 def dot(a, b, dims):
@@ -277,20 +278,6 @@
     ghs[...] = ghb[oth].astype(BF16)
     g_x = send(ghs, ghr, sib)
 
-    def to_grad(plane, source):
-        @pl.loop(0, 4)
-        def _(i):
-            cols = pl.ds(pl.multiple_of(i * 256, 256), 256)
-            v = (source[:, cols].astype(F32) * der[plane, :, cols]).astype(BF16)
-            cg[plane, :, cols] = v
-            cgt[plane, cols] = v.astype(F32).T.astype(BF16)
-
-    to_grad(own, ghb.at[own])
-    g_x.wait_recv()
-    to_grad(oth, ghr)
-    g_up = send(cgt.at[1], chalo.at[0], ch, f_up)
-    g_dn = send(cgt.at[0], chalo.at[1], ch, f_dn)
-
     for c in ph_near:
         c.wait_recv()
 
@@ -306,6 +293,21 @@
 
     s2 = [second(0)]
 
+    def to_grad(plane, source):
+        @pl.loop(0, 4)
+        def _(i):
+            cols = pl.ds(pl.multiple_of(i * 256, 256), 256)
+            v = (source[:, cols].astype(F32) * der[plane, :, cols]).astype(BF16)
+            cg[plane, :, cols] = v
+            cgt[plane, cols] = v.astype(F32).T.astype(BF16)
+
+    to_grad(own, ghb.at[own])
+    g_x.wait_recv()
+    to_grad(oth, ghr)
+    g_up = send(cgt.at[1], chalo.at[0], ch, f_up)
+    g_dn = send(cgt.at[0], chalo.at[1], ch, f_dn)
+
+
     def window_row(plane):
         return jnp.concatenate([x3t[plane, 32 * b : 32 * b + 1024] for b in range(3)], axis=1)
 
@@ -373,13 +375,13 @@
 
     wq = [send(wgp.at[f_pair(f)], wgq.at[fx], ch, f) for f in fxs]
 
+    s2.append(second(1))
     for c in s2[0]:
         c.wait_recv()
     pbuf[here[0]] = (
         pbuf[here[0]].astype(F32) + r2[0, 0].astype(F32) + r2[1, 0].astype(F32)
     ).astype(BF16)
     s3 = send(pbuf.at[here[0]], r3, yn)
-    s2.append(second(1))
 
     kq = []
     for a in range(3):
@@ -435,6 +437,25 @@
         c.wait()
     for c in sent:
         c.wait_send()
+
+
+def copy_kernel(*refs):
+    sem = refs[12]
+    loads, stores = [], []
+    for i in range(4):
+        src, held = refs[i], refs[8 + i]
+        step = src.shape[0] // PIECES[i]
+        for j in range(PIECES[i]):
+            part = pl.ds(j * step, step)
+            copy = pltpu.make_async_copy(src.at[part], held.at[part], sem.at[0, len(loads)])
+            copy.start()
+            loads.append((copy, held.at[part], refs[4 + i].at[part]))
+    for copy, held, dst in loads:
+        copy.wait()
+        stores.append(pltpu.make_async_copy(held, dst, sem.at[1, len(stores)]))
+        stores[-1].start()
+    for copy in stores:
+        copy.wait()
 
 
 def body(inputs, conv_kernel, proj_weight, out_grad):
@@ -486,14 +507,15 @@
         ((3, 288, 128), BF16),
         ((3, 1152, 128), BF16),
     ]
-    return pl.pallas_call(
+    out_shape = (
+        jax.ShapeDtypeStruct((128, 2, 1024), BF16),
+        jax.ShapeDtypeStruct((128, 2, 1024), BF16),
+        jax.ShapeDtypeStruct((27, 128, 128), F32),
+        jax.ShapeDtypeStruct((256, 128), F32),
+    )
+    results = pl.pallas_call(
         kernel,
-        out_shape=(
-            jax.ShapeDtypeStruct((128, 2, 1024), BF16),
-            jax.ShapeDtypeStruct((128, 2, 1024), BF16),
-            jax.ShapeDtypeStruct((27, 128, 128), F32),
-            jax.ShapeDtypeStruct((256, 128), F32),
-        ),
+        out_shape=out_shape,
         in_specs=[anywhere] * 4,
         out_specs=(anywhere,) * 4,
         scratch_shapes=[pltpu.VMEM(s, d) for s, d in shapes]
@@ -502,6 +524,14 @@
             collective_id=0, has_side_effects=True, vmem_limit_bytes=56 * 1024 * 1024
         ),
     )(inputs, conv_kernel, proj_weight, out_grad)
+    return pl.pallas_call(
+        copy_kernel,
+        out_shape=out_shape,
+        in_specs=[anywhere] * 4,
+        out_specs=(anywhere,) * 4,
+        scratch_shapes=[pltpu.VMEM(o.shape, o.dtype) for o in out_shape]
+        + [pltpu.SemaphoreType.DMA((2, sum(PIECES)))],
+    )(*results)
 
 
 def solution(mesh):

time: 95.9 us -> 90.5 us (0.944)
  local copies, waits for them, and re-layouts: 6.39 us -> 0 us
  Pallas kernels: 88.3 us -> 89.7 us
    unnamed x8 -> x0, local copies, waits for them, and re-layouts: 6.39 us -> none
    pallas_call x1 -> x2, Pallas kernels: 88.3 us -> 89.7 us  [the longest x1 86.9 us: body(): pl.pallas_call(kernel, out_shape=out_shape, in_specs=[anywhere] * 4, out_...]
where the time goes in v4:
time: 90.5 us; the launch traced here: 90.3 us
  Pallas kernels  89.7 us (99%)
    pallas_call x1, Pallas kernels, body(): pl.pallas_call(kernel, out_shape=out_shape, in_specs=[anywhere] * 4, out_...  86.9 us
    pallas_call x1, Pallas kernels, body(): pl.pallas_call(copy_kernel, out_shape=out_shape, in_specs=[anywhere] * 4,...  2.76 us

profile of v4, /device:TPU:0, one launch (start us, length us, event | category | flops | bytes accessed | tf_op | source)
XLA Modules:
  0.0 90.3 jit_solution(352789071874344192)
XLA Ops:
  0.6 86.9 %shard_map.75 = (bf16[128,2,1024]{2,1,0:T(2,128)(2,1)}, bf16[128,2,1024]{2,1,0:T(2,128)(2,1)}, f32[27,128,128]{2,1,0:T(8,128)}, f32[256,128]{1,0:T(8,128)}) custom-call(bf16[128,2,1024]{2,1,0:T(2,128)(2,1)} %x_in.1, bf16[27,128,128]{2,1,0:T(8,128)(2,1)} %k_in.1, bf16[256,128]{1,0:T(8,128)(2,1)} %w_in_ref.1, bf16[128,2,1024]{2,1,0:T(2,128)(2,1)} %o_in.1), custom_call_target="tpu_custom_call" | custom-call | tf_op jit(solution)/shard_map/pallas_call | solution.py:516
  87.6 2.8 %shard_map.76 = (bf16[128,2,1024]{2,1,0:T(2,128)(2,1)}, bf16[128,2,1024]{2,1,0:T(2,128)(2,1)}, f32[27,128,128]{2,1,0:T(8,128)}, f32[256,128]{1,0:T(8,128)}) custom-call(bf16[128,2,1024]{2,1,0:T(2,128)(2,1)} %get-tuple-element.8.refs_0_, bf16[128,2,1024]{2,1,0:T(2,128)(2,1)} %get-tuple-element.9.refs_1_, f32[27,128,128]{2,1,0:T(8,128)} %get-tuple-element.10.refs_2_, ...), custom_call_target="tpu_custom_call" | custom-call | tf_op jit(solution)/shard_map/pallas_call | solution.py:527

commit v5 on v4

--- a/solution.py
+++ b/solution.py
@@ -376,13 +376,6 @@
     wq = [send(wgp.at[f_pair(f)], wgq.at[fx], ch, f) for f in fxs]
 
     s2.append(second(1))
-    for c in s2[0]:
-        c.wait_recv()
-    pbuf[here[0]] = (
-        pbuf[here[0]].astype(F32) + r2[0, 0].astype(F32) + r2[1, 0].astype(F32)
-    ).astype(BF16)
-    s3 = send(pbuf.at[here[0]], r3, yn)
-
     kq = []
     for a in range(3):
         ky[a].wait_recv()
@@ -391,21 +384,13 @@
             send(kgall.at[a, x_slice(fi)], kgall.at[a, x_slice(fi)], ch, f) for f in fxs
         ]
 
-    g_up.wait_recv()
-    g_dn.wait_recv()
-    spread(c3t, 0, chalo.at[0], False, first)
-    spread(c3t, 3, chalo.at[1], False, last)
-
-    for plane in range(2):
-        @pl.loop(0, 4)
-        def _(i):
-            cols = pl.ds(pl.multiple_of(i * 256, 256), 256)
-            wins = windows(c3t, 3 * plane, i, back)
-            taps = k_ref[18 * (1 - plane) : 18 * (1 - plane) + 9].reshape(1152, 128)
-            v = dot(jnp.concatenate(wins, axis=1), taps, NN)
-            ig_out[:, plane, cols] = (ghb[plane, :, cols] + v.T).astype(BF16)
-
-    ig_store = local(ig_out, ig_res, 4)
+    for c in s2[0]:
+        c.wait_recv()
+    pbuf[here[0]] = (
+        pbuf[here[0]].astype(F32) + r2[0, 0].astype(F32) + r2[1, 0].astype(F32)
+    ).astype(BF16)
+    s3 = send(pbuf.at[here[0]], r3, yn)
+
     total = wgf[f_pair(fi)]
     for c in wq:
         c.wait_recv()
@@ -415,6 +400,21 @@
     wgy[...] = wgf[fy].astype(BF16)
     wy = send(wgy, wgz, ch, fy)
 
+    g_up.wait_recv()
+    g_dn.wait_recv()
+    spread(c3t, 0, chalo.at[0], False, first)
+    spread(c3t, 3, chalo.at[1], False, last)
+
+    for plane in range(2):
+        @pl.loop(0, 4)
+        def _(i):
+            cols = pl.ds(pl.multiple_of(i * 256, 256), 256)
+            wins = windows(c3t, 3 * plane, i, back)
+            taps = k_ref[18 * (1 - plane) : 18 * (1 - plane) + 9].reshape(1152, 128)
+            v = dot(jnp.concatenate(wins, axis=1), taps, NN)
+            ig_out[:, plane, cols] = (ghb[plane, :, cols] + v.T).astype(BF16)
+
+    ig_store = local(ig_out, ig_res, 4)
     wy.wait_recv()
     wg_out[...] = wgf[fi] + wgz[...].astype(F32)
     stores = [ig_store, local(wg_out, wg_res, 5)]

time: 90.5 us -> 90.5 us (level)
  no operation moved by 1% of the time
where the time goes in v5:
time: 90.5 us; the launch traced here: 90.3 us
  Pallas kernels  89.7 us (99%)
    pallas_call x1, Pallas kernels, body(): pl.pallas_call(kernel, out_shape=out_shape, in_specs=[anywhere] * 4, out_...  86.9 us
    pallas_call x1, Pallas kernels, body(): pl.pallas_call(copy_kernel, out_shape=out_shape, in_specs=[anywhere] * 4,...  2.76 us

profile of v5, /device:TPU:0, one launch (start us, length us, event | category | flops | bytes accessed | tf_op | source)
XLA Modules:
  0.0 90.3 jit_solution(16808609929754878922)
XLA Ops:
  0.6 86.9 %shard_map.75 = (bf16[128,2,1024]{2,1,0:T(2,128)(2,1)}, bf16[128,2,1024]{2,1,0:T(2,128)(2,1)}, f32[27,128,128]{2,1,0:T(8,128)}, f32[256,128]{1,0:T(8,128)}) custom-call(bf16[128,2,1024]{2,1,0:T(2,128)(2,1)} %x_in.1, bf16[27,128,128]{2,1,0:T(8,128)(2,1)} %k_in.1, bf16[256,128]{1,0:T(8,128)(2,1)} %w_in_ref.1, bf16[128,2,1024]{2,1,0:T(2,128)(2,1)} %o_in.1), custom_call_target="tpu_custom_call" | custom-call | tf_op jit(solution)/shard_map/pallas_call | solution.py:516
  87.6 2.8 %shard_map.76 = (bf16[128,2,1024]{2,1,0:T(2,128)(2,1)}, bf16[128,2,1024]{2,1,0:T(2,128)(2,1)}, f32[27,128,128]{2,1,0:T(8,128)}, f32[256,128]{1,0:T(8,128)}) custom-call(bf16[128,2,1024]{2,1,0:T(2,128)(2,1)} %get-tuple-element.8.refs_0_, bf16[128,2,1024]{2,1,0:T(2,128)(2,1)} %get-tuple-element.9.refs_1_, f32[27,128,128]{2,1,0:T(8,128)} %get-tuple-element.10.refs_2_, ...), custom_call_target="tpu_custom_call" | custom-call | tf_op jit(solution)/shard_map/pallas_call | solution.py:527
